TPU v7x, 1024 devices: a whole 4x8x16 slice. The times are simulated.
1024 devices in a mesh: ctx: 32 (over z, core), head: 32 (over y, x).
Axes of the slice: x: 4, y: 8, z: 16, core: 2. Of those that a mesh axis runs over, the one named last changes fastest.
Arguments:
- queries: bfloat16 [98304, 4096], P(('ctx', 'head')), may hold values from -6 to 6
- keys: bfloat16 [98304, 4096], P(('ctx', 'head')), may hold values from -6 to 6
- values: bfloat16 [98304, 4096], P(('ctx', 'head')), may hold values from -6 to 6
- log_decay: bfloat16 [98304, 32], P(('ctx', 'head')), as said below
- gain: float32 [4096], P('head'), may hold values from 0.1 to 1.9
- doc_starts: int32 [9], replicated, may hold values from 0 to 98304, as said below
Outputs:
- attended: bfloat16 [98304, 4096], P(('ctx', 'head'))
Inputs may be any that keep to these rules, and one draw needn't show every extreme that they name: doc_starts begins with 0, ends with 98304 and rises strictly; the first document holds at least 61440 tokens. `log_decay`: entries are at most 0.
All inputs are finite; a program needn't handle non-finite values.
Results may differ from a plain program's by a relative error of at most 0.0049.
Values may be sent and summed in bfloat16 or wider, within the bound.
No kernel may reach another device: no remote copies, remote signals or barrier semaphores. Data moves between devices by JAX's collectives and lax.ppermute only.
A program may use at most 32 MiB of HBM per device.

v0:
```python
import jax
import jax.numpy as jnp
from jax import lax
from jax.sharding import PartitionSpec as P

E = 128


block_cap = 512


def carried_in(value, axis, join, neutral):
    count, mine = (lax.axis_size(axis), lax.axis_index(axis))
    pieces = jax.tree.map(lambda part: lax.all_gather(part, axis), value)
    total = jax.tree.map(
        lambda part, zero: jnp.full_like(part, 0) + jnp.asarray(zero, part.dtype), value, neutral
    )

    def hop(position, total):
        longer = join(total, jax.tree.map(lambda part: part[position], pieces))
        return jax.tree.map(lambda new, old: jnp.where(position < mine, new, old), longer, total)

    return lax.fori_loop(0, count - 1, hop, total)


def combine(earlier, later):
    return (earlier[0] * later[0], later[0][:, None, None] * earlier[1] + later[1])


def per_device(queries, keys, values, log_decay, gain, doc_starts):
    heads = gain.shape[0] // E
    q_group = lax.all_to_all(queries, "head", split_axis=1, concat_axis=0, tiled=True)
    k_group, v_group, g_group = (
        lax.all_to_all(keys, "head", split_axis=1, concat_axis=0, tiled=True),
        lax.all_to_all(values, "head", split_axis=1, concat_axis=0, tiled=True),
        lax.all_to_all(log_decay, "head", split_axis=1, concat_axis=0, tiled=True),
    )
    group = q_group.shape[0]
    block = min(block_cap, group)
    nblk = group // block
    ndoc = doc_starts.shape[0] - 1
    offset = lax.axis_index("ctx") * group
    token_positions = offset + jnp.arange(group, dtype=jnp.int32)
    doc_id = jnp.sum(
        (token_positions[:, None] >= doc_starts[None, 1:ndoc]).astype(jnp.int32), axis=1
    )
    is_start = jnp.any(token_positions[:, None] == doc_starts[None, 0:ndoc], axis=1)
    qb = q_group.reshape(nblk, block, heads, E)
    kb = k_group.reshape(nblk, block, heads, E)
    vb = v_group.reshape(nblk, block, heads, E)
    gb = g_group.reshape(nblk, block, heads)
    docb = doc_id.reshape(nblk, block)
    startb = is_start.reshape(nblk, block)
    rows = jnp.arange(block, dtype=jnp.int32)

    def local_block(carry, item):
        acc_a, acc_s = carry
        qx, kx, vx, gx, dx, sx = item
        cum = jnp.cumsum(gx.astype(jnp.float32), axis=0)
        opened = jnp.cumsum(sx.astype(jnp.int32)) == 0
        mask = (rows[None, :] <= rows[:, None]) & (dx[:, None] == dx[None, :])
        cum_t = cum.T
        diff = cum_t[:, :, None] - cum_t[:, None, :]
        decay = jnp.where(mask[None], jnp.exp(jnp.where(mask[None], diff, 0.0)), 0.0)
        scores = jnp.einsum("thd,jhd->htj", qx, kx, preferred_element_type=jnp.float32)
        weights = (scores * decay).astype(jnp.bfloat16)
        intra = jnp.einsum("htj,jhe->the", weights, vx, preferred_element_type=jnp.float32)
        last = cum[-1]
        tail = jnp.exp(last[None, :] - cum) * (dx == dx[-1])[:, None].astype(jnp.float32)
        scaled_keys = (kx.astype(jnp.float32) * tail[:, :, None]).astype(jnp.bfloat16)
        summary = jnp.einsum("jhe,jhf->hef", scaled_keys, vx, preferred_element_type=jnp.float32)
        keep = jnp.exp(last) * opened[-1].astype(jnp.float32)
        reach = jnp.exp(cum) * opened[:, None].astype(jnp.float32)
        updated = (acc_a * keep, keep[:, None, None] * acc_s + summary)
        return (updated, (intra, reach, acc_a, acc_s))

    start_carry = (jnp.ones((heads,), jnp.float32), jnp.zeros((heads, E, E), jnp.float32))
    device_sum, stacked = lax.scan(local_block, start_carry, (qb, kb, vb, gb, docb, startb))
    intra, reach, pre_a, pre_s = stacked
    dev_a, dev_s = device_sum
    enter_a, enter_s = carried_in((dev_a, dev_s), "ctx", combine, start_carry)
    block_in = pre_a[:, :, None, None] * enter_s[None] + pre_s
    scaled_q = qb.astype(jnp.float32) * reach[..., None]
    inter = jnp.einsum("bthe,bhef->bthf", scaled_q, block_in, precision=lax.Precision.HIGHEST)
    attn = intra + inter
    meansq = jnp.mean(attn * attn, axis=-1, keepdims=True)
    normed = attn * lax.rsqrt(meansq + 1e-05) * gain.reshape(heads, E)[None, None]
    result = normed.astype(jnp.bfloat16).reshape(group, heads * E)
    return lax.all_to_all(result, "head", split_axis=0, concat_axis=1, tiled=True)


def solution(mesh):
    in_specs = (
        P(("ctx", "head"), None),
        P(("ctx", "head"), None),
        P(("ctx", "head"), None),
        P(("ctx", "head"), None),
        P("head"),
        P(),
    )
    out_specs = P(("ctx", "head"), None)
    return jax.shard_map(
        per_device, mesh=mesh, in_specs=in_specs, out_specs=out_specs, check_vma=False
    )
```

profile of v0, /device:TPU:1, one launch (start us, length us, event | category | flops | bytes accessed | tf_op | source)
XLA Modules:
  0.0 352.0 jit_solution(5220226236983961802)
XLA Ops:
  7.9 10.5 %all-to-all-start = ((bf16[96,32,1]{0,2,1:T(2,128)(2,1)}), bf16[96,32,1]{0,2,1:T(2,128)(2,1)S(1)}, u32[]{:S(2)}, u32[]{:S(2)}) async-start(bf16[96,32,1]{0,2,1:T(2,128)(2,1)} %copy.67), calls=%async_computation | async-start | bytes 32768 | tf_op jit(solution)/shard_map/all_to_all | solution.py:36
  19.5 7.5 %all-to-all-done = bf16[96,32,1]{0,2,1:T(2,128)(2,1)S(1)} async-done(((bf16[96,32,1]{0,2,1:T(2,128)(2,1)}), bf16[96,32,1]{0,2,1:T(2,128)(2,1)S(1)}, u32[]{:S(2)}, u32[]{:S(2)}) %all-to-all-start) | async-done | bytes 6176 | tf_op jit(solution)/shard_map/all_to_all | solution.py:36
  27.0 3.9 %all-to-all-start.3 = ((bf16[96,32,128]{2,0,1:T(8,128)(2,1)}), bf16[96,32,128]{2,0,1:T(8,128)(2,1)S(1)}, u32[]{:S(2)}, u32[]{:S(2)}) async-start(bf16[96,32,128]{2,0,1:T(8,128)(2,1)} %copy_bitcast_fusion.1), calls=%async_computation.3 | async-start | bytes 1572864 | tf_op jit(solution)/shard_map/all_to_all | solution.py:32
  31.9 14.2 %all-to-all-done.3 = bf16[96,32,128]{2,0,1:T(8,128)(2,1)S(1)} async-done(((bf16[96,32,128]{2,0,1:T(8,128)(2,1)}), bf16[96,32,128]{2,0,1:T(8,128)(2,1)S(1)}, u32[]{:S(2)}, u32[]{:S(2)}) %all-to-all-start.3) | async-done | bytes 786464 | tf_op jit(solution)/shard_map/all_to_all | solution.py:32
  46.1 4.3 %all-to-all-start.1 = ((bf16[96,32,128]{2,0,1:T(8,128)(2,1)}), bf16[96,32,128]{2,0,1:T(8,128)(2,1)S(1)}, u32[]{:S(2)}, u32[]{:S(2)}) async-start(bf16[96,32,128]{2,0,1:T(8,128)(2,1)} %copy_bitcast_fusion.3), calls=%async_computation.1 | async-start | bytes 1572864 | tf_op jit(solution)/shard_map/all_to_all | solution.py:34
  51.5 14.0 %all-to-all-done.1 = bf16[96,32,128]{2,0,1:T(8,128)(2,1)S(1)} async-done(((bf16[96,32,128]{2,0,1:T(8,128)(2,1)}), bf16[96,32,128]{2,0,1:T(8,128)(2,1)S(1)}, u32[]{:S(2)}, u32[]{:S(2)}) %all-to-all-start.1) | async-done | bytes 786464 | tf_op jit(solution)/shard_map/all_to_all | solution.py:34
  65.5 4.5 %all-to-all-start.2 = ((bf16[96,32,128]{2,0,1:T(8,128)(2,1)}), bf16[96,32,128]{2,0,1:T(8,128)(2,1)S(1)}, u32[]{:S(2)}, u32[]{:S(2)}) async-start(bf16[96,32,128]{2,0,1:T(8,128)(2,1)} %copy_bitcast_fusion.2), calls=%async_computation.2 | async-start | bytes 1572864 | tf_op jit(solution)/shard_map/all_to_all | solution.py:35
  70.6 14.5 %all-to-all-done.2 = bf16[96,32,128]{2,0,1:T(8,128)(2,1)S(1)} async-done(((bf16[96,32,128]{2,0,1:T(8,128)(2,1)}), bf16[96,32,128]{2,0,1:T(8,128)(2,1)S(1)}, u32[]{:S(2)}, u32[]{:S(2)}) %all-to-all-start.2) | async-done | bytes 786464 | tf_op jit(solution)/shard_map/all_to_all | solution.py:35
  85.2 53.6 %while.35 = (s32[]{:T(128)}, f32[1]{0:T(128)}, f32[1,128,128]{2,1,0:T(8,128)S(1)}, f32[6,512,1,128]{1,3,2,0:T(8,128)}, f32[6,512,1]{1,0,2:T(8,128)S(1)}, /*index...) while((s32[]{:T(128)}, f32[1]{0:T(128)}, ...), condition=%wide.region_7.8_spmd.clone, body=%wide.region_2.7_spmd.clone.sunk | while | flops 153490464 | bytes 1239627 | solution.py:78
  141.4 83.0 %all-reduce = f32[32]{0:T(128)S(1)} all-reduce(f32[32]{0:T(128)S(1)} %dynamic-update-slice), channel_id=2, replica_groups=mesh['ctx'=32,'head'=32] {'ctx'}, use_global_device_ids=true, to_apply=%add | all-reduce | flops 32 | bytes 256
  224.4 15.9 %all-gather.4.cloned.1.call-done = f32[32,128,128]{2,1,0:T(8,128)} async-done(((f32[1,128,128]{2,1,0:T(8,128)}), f32[32,128,128]{2,1,0:T(8,128)}) %all-gather.4.cloned.1.call-update) | async-done | bytes 2097168 | tf_op jit(solution)/shard_map/all_gather | solution.py:14
  240.3 69.0 %while.36 = (s32[]{:T(128)}, f32[1,128,128]{2,1,0:T(8,128)S(1)}, s32[]{:T(128)}, f32[32,1]{0,1:T(1,128)S(1)}, f32[32,1,128,128]{3,2,1,0:T(8,128)}, /*index=5*/s32[]{:T(128)}, s32[]{:T(128)}) while((s32[]{:T(128)}, f32[1,128,128]{2,1,0:T(8,128)S(1)}, s32[]{:T(128)}, f32[32,1]{0,1:T(1,128)S(1)}, f32[32,1,128,128]{3,2,1,0:T(8,128)}, ...), condition=%wide.region_9.10_spmd.clone, body=%wide.region_8.9_spmd.clone.sunk | while | flops 65540 | bytes 196725 | solution.py:23
  241.0 1.5 fusion.71
  243.2 1.5 fusion.71
  245.4 1.5 fusion.71
  247.6 1.5 fusion.71
  252.1 1.5 fusion.71
  256.6 1.5 fusion.71
  261.0 1.5 fusion.71
  263.2 1.5 fusion.71
  265.5 1.5 fusion.71
  267.7 1.5 fusion.71
  269.9 1.5 fusion.71
  272.1 1.5 fusion.71
  274.4 1.5 fusion.71
  276.6 1.5 fusion.71
  278.8 1.5 fusion.71
  281.0 1.5 fusion.71
  283.3 1.5 fusion.71
  285.5 1.5 fusion.71
  309.3 3.7 %multiply_reduce_fusion = (f32[6,512]{1,0:T(8,128)S(1)}, f32[6,512,1,128]{1,3,0,2:T(8,128)S(1)}) fusion(bf16[6,512,128]{2,1,0:T(8,128)(2,1)S(1)} %bitcast.184, f32[6,512]{1,0:T(8,128)S(1)} %bitcast.198, f32[6,1,128,128]{3,2,1,0:T(8,128)} %get-tuple-element.181, f32[128,128]{1,0:T(8,128)S(1)} %bitcast.188, f32[6]{0:T(128)S(1)} %bitcast.201, ...), kind=kOutput, calls=%fused_computation.55 | convolution fusion | flops 606139392 | bytes 4415512 | tf_op jit(solution)/shard_map/bthe,bhef->bthf/dot_general | solution.py:84
  313.8 30.4 %all_to_all.83 = bf16[32,96,128]{2,1,0:T(8,128)(2,1)S(1)} all-to-all(bf16[32,96,128]{2,1,0:T(8,128)(2,1)S(1)} %bitcast.185), channel_id=1, replica_groups=mesh['ctx'=32,'head'=32] {'head'}, dimensions={0} | all-to-all | bytes 1572864 | tf_op jit(solution)/shard_map/all_to_all | solution.py:89
  (239 shorter events, 92.0 us)
Async XLA Ops:
  6.5 11.9 %copy-start = (bf16[96,4096]{1,0:T(8,128)(2,1)S(1)}, bf16[96,4096]{1,0:T(8,128)(2,1)}, u32[]{:S(2)}) copy-start(bf16[96,4096]{1,0:T(8,128)(2,1)} %param.10) | copy-start | bytes 2359300
  7.9 19.0 %all-to-all-start = ((bf16[96,32,1]{0,2,1:T(2,128)(2,1)}), bf16[96,32,1]{0,2,1:T(2,128)(2,1)S(1)}, u32[]{:S(2)}, u32[]{:S(2)}) async-start(bf16[96,32,1]{0,2,1:T(2,128)(2,1)} %copy.67), calls=%async_computation | async-start | bytes 32768 | tf_op jit(solution)/shard_map/all_to_all | solution.py:36
  18.4 12.4 %copy-start.2 = (bf16[96,4096]{1,0:T(8,128)(2,1)S(1)}, bf16[96,4096]{1,0:T(8,128)(2,1)}, u32[]{:S(2)}) copy-start(bf16[96,4096]{1,0:T(8,128)(2,1)} %param.11) | copy-start | bytes 2359300
  27.0 19.2 %all-to-all-start.3 = ((bf16[96,32,128]{2,0,1:T(8,128)(2,1)}), bf16[96,32,128]{2,0,1:T(8,128)(2,1)S(1)}, u32[]{:S(2)}, u32[]{:S(2)}) async-start(bf16[96,32,128]{2,0,1:T(8,128)(2,1)} %copy_bitcast_fusion.1), calls=%async_computation.3 | async-start | bytes 1572864 | tf_op jit(solution)/shard_map/all_to_all | solution.py:32
  30.9 19.6 %copy-start.3 = (bf16[96,4096]{1,0:T(8,128)(2,1)S(1)}, bf16[96,4096]{1,0:T(8,128)(2,1)}, u32[]{:S(2)}) copy-start(bf16[96,4096]{1,0:T(8,128)(2,1)} %param.12) | copy-start | bytes 2359300
  46.1 19.4 %all-to-all-start.1 = ((bf16[96,32,128]{2,0,1:T(8,128)(2,1)}), bf16[96,32,128]{2,0,1:T(8,128)(2,1)S(1)}, u32[]{:S(2)}, u32[]{:S(2)}) async-start(bf16[96,32,128]{2,0,1:T(8,128)(2,1)} %copy_bitcast_fusion.3), calls=%async_computation.1 | async-start | bytes 1572864 | tf_op jit(solution)/shard_map/all_to_all | solution.py:34
  50.4 19.7 %copy-start.4 = (s32[9]{0:T(128)S(1)}, s32[9]{0:T(128)}, u32[]{:S(2)}) copy-start(s32[9]{0:T(128)} %param.15) | copy-start | bytes 112
  65.5 19.6 %all-to-all-start.2 = ((bf16[96,32,128]{2,0,1:T(8,128)(2,1)}), bf16[96,32,128]{2,0,1:T(8,128)(2,1)S(1)}, u32[]{:S(2)}, u32[]{:S(2)}) async-start(bf16[96,32,128]{2,0,1:T(8,128)(2,1)} %copy_bitcast_fusion.2), calls=%async_computation.2 | async-start | bytes 1572864 | tf_op jit(solution)/shard_map/all_to_all | solution.py:35
  70.0 170.3 %all-gather.4.cloned.1.call-start = ((), (), s32[]{:S(2)}) async-start(), calls=%async_computation.5 | async-start | bytes 2162688 | tf_op jit(solution)/shard_map/all_gather | solution.py:14
  138.8 0.6 copy-start.1
  309.3 3.7 %copy-start.5 = (f32[128]{0:T(128)S(1)}, f32[128]{0:T(128)}, u32[]{:S(2)}) copy-start(f32[128]{0:T(128)} %param.14) | copy-start | bytes 1540
Sparse Core Ops, SparseCore 0:
  139.6 100.7 all-gather.3
where the time goes:
time: 355 us; the launch traced here: 352 us
  blocking collectives  113 us (32%)
  waiting for transfers between devices  66.2 us (19%)
  other arithmetic  62.2 us (18%)
  local copies, waits for them, and re-layouts  47.6 us (13%)
  starting transfers between devices  23.2 us (7%)
  matrix products  13.6 us (4%)
  between operations  13.6 us (4%)
  loops' own time  12.1 us (3%)
    unnamed x1, blocking collectives  83 us
    select_n x31, other arithmetic, hop(): jnp.where(position < mine, new, old)  47.9 us
    all_to_all x1, blocking collectives, per_device(): lax.all_to_all(result, 'head', split_axis=0, concat_axis=1, tiled=True)  30.4 us
    dynamic_slice x31, local copies, waits for them, and re-layouts, hop(): longer = join(total, jax.tree.map(lambda part: part[position], pieces))  20.6 us
    all_gather x1, waiting for transfers between devices, carried_in(): pieces = jax.tree.map(lambda part: lax.all_gather(part, axis), value)  15.9 us
    all_to_all x1, waiting for transfers between devices, per_device(): lax.all_to_all(values, 'head', split_axis=1, concat_axis=0, tiled=True)  14.5 us
    all_to_all x1, waiting for transfers between devices, per_device(): lax.all_to_all(queries, 'head', split_axis=1, concat_axis=0, tiled=True)  14.2 us
    all_to_all x1, waiting for transfers between devices, per_device(): lax.all_to_all(keys, 'head', split_axis=1, concat_axis=0, tiled=True)  14 us
  transfers between devices with their start and end apart: 5, of which 5 were waited for; matrix products, arithmetic and copies ran while one was open for 2% of the time, Pallas kernels for 0%

commit v1 on v0

v1 whole, which is shorter than its diff:
```python
import functools

import jax
import jax.numpy as jnp
from jax import lax
from jax.experimental import pallas as pl
from jax.experimental.pallas import tpu as pltpu
from jax.sharding import Mesh, PartitionSpec as P

E = 128
HALF = E // 2
PAD = 8
AXES = ("z", "core", "y", "x")
PLANE = ("core", "y", "x")
F32, BF16 = jnp.float32, jnp.bfloat16
VMEM = pl.BlockSpec(memory_space=pltpu.VMEM)
ANY = pl.BlockSpec(memory_space=pl.ANY)
SMEM = pl.BlockSpec(memory_space=pltpu.SMEM)


def started(position, starts_ref):
    count = jnp.zeros_like(position)
    for i in range(starts_ref.shape[0] - 1):
        count = count + (position >= starts_ref[i]).astype(jnp.int32)
    return count


def cumulative(decay_ref):
    tokens = decay_ref.shape[0]
    i = lax.broadcasted_iota(jnp.int32, (tokens, tokens), 0)
    j = lax.broadcasted_iota(jnp.int32, (tokens, tokens), 1)
    lower = (i >= j).astype(BF16)
    return jnp.dot(lower, decay_ref[...], preferred_element_type=F32)


def three_parts(value):
    high = value.astype(BF16).astype(F32)
    middle = (value - high).astype(BF16).astype(F32)
    return high, middle, (value - high - middle).astype(BF16).astype(F32)


def column(h):
    return slice(h * E, (h + 1) * E)


def summarize(first_ref, starts_ref, k_ref, v_ref, decay_ref, gain_ref, out_ref):
    tokens, heads = decay_ref.shape
    first = first_ref[0]
    position = first + lax.broadcasted_iota(jnp.int32, (tokens, 1), 0)
    at_end = started(first + tokens - 1, starts_ref)
    cum = cumulative(decay_ref)
    last = cum[tokens - 1 :, :]
    tail = jnp.where(started(position, starts_ref) == at_end, jnp.exp(last - cum), 0.0)
    open_all = at_end == started(first - 1, starts_ref)
    keep = three_parts(jnp.where(open_all, jnp.exp(last), 0.0))
    gains = three_parts(gain_ref[...])
    row = lax.broadcasted_iota(jnp.int32, (PAD, E), 0)
    base = jnp.zeros((PAD, E), F32)
    for i in range(3):
        base = jnp.where(row == 3 + i, jnp.broadcast_to(gains[i], (PAD, E)), base)
    for h in range(heads):
        scaled = (k_ref[:, column(h)].astype(F32) * tail[:, h : h + 1]).astype(BF16)
        state = lax.dot_general(
            scaled, v_ref[:, column(h)], (((0,), (0,)), ((), ())), preferred_element_type=F32
        ).astype(BF16)
        extra = base
        for i in range(3):
            extra = jnp.where(row == i, jnp.broadcast_to(keep[i][:, h : h + 1], (PAD, E)), extra)
        for c in range(2):
            out_ref[c * heads + h, 0:HALF, :] = state[c * HALF : (c + 1) * HALF]
            out_ref[c * heads + h, HALF : HALF + PAD, :] = extra.astype(BF16)


def within(first_ref, starts_ref, q_ref, k_ref, v_ref, decay_ref, out_ref, done_ref, *, heads):
    done_ref[...] = jnp.zeros_like(done_ref)
    tokens = decay_ref.shape[0]
    first = first_ref[0]
    i = lax.broadcasted_iota(jnp.int32, (tokens, tokens), 0)
    j = lax.broadcasted_iota(jnp.int32, (tokens, tokens), 1)
    mask = (i >= j) & (started(first + i, starts_ref) == started(first + j, starts_ref))
    cum = cumulative(decay_ref)
    across = cum.T
    for n, h in enumerate(heads):
        scores = lax.dot_general(
            q_ref[:, column(h)], k_ref[:, column(h)], (((1,), (1,)), ((), ())), preferred_element_type=F32
        )
        decay = jnp.exp(jnp.where(mask, cum[:, h : h + 1] - across[h : h + 1, :], -1e30))
        weights = (scores * decay).astype(BF16)
        out_ref[:, column(n)] = jnp.dot(weights, v_ref[:, column(h)], preferred_element_type=F32)


def kept(ref, n):
    parts = ref[n, HALF : HALF + PAD, :].astype(F32)
    return parts[0:1] + parts[1:2] + parts[2:3]


def plane_total(got_ref, _, out_ref, gain_ref):
    sources, heads = got_ref.shape[0], gain_ref.shape[0]

    def one(n, carry):
        state, keep = carry
        mine = kept(got_ref, n)
        return mine * state + got_ref[n, 0:HALF, :].astype(F32), mine * keep

    state, keep = lax.fori_loop(
        0, sources, one, (jnp.zeros((HALF, E), F32), jnp.ones((1, E), F32)), unroll=8
    )
    row = lax.broadcasted_iota(jnp.int32, (PAD, E), 0)
    extra = jnp.zeros((PAD, E), F32)
    for i, part in enumerate(three_parts(keep)):
        extra = jnp.where(row == i, jnp.broadcast_to(part, (PAD, E)), extra)
    state, extra = state.astype(BF16), extra.astype(BF16)
    for z in range(out_ref.shape[0]):
        out_ref[z, 0:HALF, :] = state
        out_ref[z, HALF : HALF + PAD, :] = extra
    for h in range(heads):
        parts = got_ref[h, HALF : HALF + PAD, :].astype(F32)
        gain_ref[h : h + 1, :] = parts[3:4] + parts[4:5] + parts[5:6]


def entering(plane_ref, planes_ref, got_ref, _, out_ref):
    def earlier(n, state):
        return kept(planes_ref, n) * state + planes_ref[n, 0:HALF, :].astype(F32)

    def one(n, state):
        out_ref[n] = state.astype(BF16)
        return kept(got_ref, n) * state + got_ref[n, 0:HALF, :].astype(F32)

    state = lax.fori_loop(0, plane_ref[0], earlier, jnp.zeros((HALF, E), F32))
    lax.fori_loop(0, got_ref.shape[0], one, state, unroll=8)


def finish(first_ref, starts_ref, q_ref, decay_ref, *refs):
    *within_refs, enter_ref, gain_ref, out_ref = refs
    tokens, heads = decay_ref.shape
    first = first_ref[0]
    position = first + lax.broadcasted_iota(jnp.int32, (tokens, 1), 0)
    opened = started(position, starts_ref) == started(first - 1, starts_ref)
    reach = jnp.where(opened, jnp.exp(cumulative(decay_ref)), 0.0)
    places = [(ref, n) for ref in within_refs for n in range(ref.shape[1] // E)]
    for h in range(heads):
        ref, n = places[h]
        state = jnp.concatenate([enter_ref[h], enter_ref[heads + h]], axis=0)
        inter = jnp.dot(q_ref[:, column(h)], state, preferred_element_type=F32)
        attn = ref[:, column(n)] + inter * reach[:, h : h + 1]
        meansq = jnp.mean(attn * attn, axis=-1, keepdims=True)
        normed = attn * lax.rsqrt(meansq + 1e-05) * gain_ref[h : h + 1, :]
        out_ref[:, column(h)] = normed.astype(BF16)


def call(kernel, out, specs, name, flops, nbytes):
    return pl.pallas_call(
        kernel,
        out_shape=out,
        in_specs=specs,
        out_specs=jax.tree.map(lambda _: VMEM, out),
        name=name,
        cost_estimate=pl.CostEstimate(flops=flops, bytes_accessed=nbytes, transcendentals=0),
    )


def shared(heads):
    cuts = (0, heads // 2, heads // 2 + heads // 4, heads)
    return [tuple(range(a, b)) for a, b in zip(cuts, cuts[1:])]


def per_device(queries, keys, values, log_decay, gain, doc_starts):
    tokens, heads = log_decay.shape
    planes = lax.axis_size("z")
    sources = 2 * heads
    first = (lax.axis_index(AXES) * tokens).astype(jnp.int32).reshape(1)
    plane = lax.axis_index("z").astype(jnp.int32).reshape(1)
    shape = jax.ShapeDtypeStruct
    tri = 2 * tokens * tokens * E
    square = 2 * tokens * E * E

    sent = call(
        summarize, shape((sources, HALF + PAD, E), BF16), [SMEM, SMEM, VMEM, VMEM, VMEM, VMEM], "summarize",
        heads * square, 3 * 2 * tokens * heads * E,
    )(first, doc_starts, keys, values, log_decay, gain.reshape(1, E))
    got = lax.all_to_all(sent, PLANE, split_axis=0, concat_axis=0, tiled=True)

    inside, done = [], []
    for s, mine in enumerate(shared(heads)):
        attn, after = call(
                functools.partial(within, heads=mine), (shape((tokens, len(mine) * E), F32), shape((8, E), F32)),
                [SMEM, SMEM, VMEM, VMEM, VMEM, VMEM], f"within{s}", 2 * len(mine) * tri, 5 * 2 * tokens * len(mine) * E,
            )(first, doc_starts, queries, keys, values, log_decay)
        inside.append(attn)
        done.append(after)

    total, gains = call(
        plane_total, (shape((planes, HALF + PAD, E), BF16), shape((heads, E), F32)), [VMEM, ANY], "plane_total",
        4 * sources * HALF * E, 2 * sources * (HALF + PAD) * E,
    )(got, done[0])
    totals = lax.all_to_all(total, "z", split_axis=0, concat_axis=0, tiled=True)
    enter = call(
        entering, shape((sources, HALF, E), BF16), [SMEM, VMEM, VMEM, ANY], "entering",
        4 * sources * HALF * E, 4 * sources * HALF * E,
    )(plane, totals, got, done[1])
    mine = lax.all_to_all(enter, PLANE, split_axis=0, concat_axis=0, tiled=True)
    return call(
        finish, shape((tokens, heads * E), BF16), [SMEM, SMEM] + [VMEM] * (4 + len(inside)), "finish",
        heads * square, 10 * tokens * heads * E,
    )(first, doc_starts, queries, log_decay, *inside, mine, gains)


def solution(mesh):
    ctx, heads = mesh.devices.shape
    split = Mesh(mesh.devices.reshape(ctx // 2, 2, heads // 4, 4), AXES)
    rows = P(AXES, None)
    return jax.shard_map(
        per_device,
        mesh=split,
        in_specs=(rows, rows, rows, rows, P(("y", "x")), P()),
        out_specs=rows,
        check_vma=False,
    )
```

time: 355 us -> 135 us (0.38)
  blocking collectives: 113 us -> 0 us
  other arithmetic: 62.2 us -> 0 us
  local copies, waits for them, and re-layouts: 47.6 us -> 4.12 us
  Pallas kernels: 0 us -> 27 us
  starting transfers between devices: 23.2 us -> 39.2 us
  matrix products: 13.6 us -> 0 us
  between operations: 13.6 us -> 0.03 us
  loops' own time: 12.1 us -> 0 us
    unnamed x1 -> x0, blocking collectives: 83 us -> none
    select_n x31 -> x0, other arithmetic: 47.9 us -> none  [hop(): jnp.where(position < mine, new, old)]
    all_to_all x1 -> x0, blocking collectives: 30.4 us -> none  [per_device(): lax.all_to_all(result, 'head', split_axis=0, concat_axis=1, tiled=True)]
    pallas_call x0 -> x7, Pallas kernels: none -> 27 us  [the longest x3 12.5 us: per_device(): call(functools.partial(within, heads=mine), (shape((tokens, len(mine) * E...]
    dynamic_slice x37 -> x0, local copies, waits for them, and re-layouts: 20.6 us -> none  [the longest x31 20.6 us: hop(): longer = join(total, jax.tree.map(lambda part: part[position], pieces))]
    all_to_all x4 -> x3, starting transfers between devices: 23.2 us -> 39.2 us  [the longest x1 18.4 us: per_device(): got = lax.all_to_all(sent, PLANE, split_axis=0, concat_axis=0, tiled=True)]
    all_gather x1 -> x0, waiting for transfers between devices: 15.9 us -> none  [carried_in(): pieces = jax.tree.map(lambda part: lax.all_gather(part, axis), value)]
    slice x31 -> x0, local copies, waits for them, and re-layouts: 15.7 us -> none  [the longest x12 7.06 us: local_block(): last = cum[-1]]
  transfers between devices with their start and end apart: 5 -> 3, of which waited for: 5 -> 3; matrix products, arithmetic and copies ran while one was open for 2% -> 0% of each run, Pallas kernels for 0% -> 9%
where the time goes in v1:
time: 135 us; the launch traced here: 134 us
  waiting for transfers between devices  64 us (47%)
  starting transfers between devices  39.2 us (29%)
  Pallas kernels  27 us (20%)
  local copies, waits for them, and re-layouts  4.12 us (3%)
    all_to_all x1, waiting for transfers between devices, per_device(): got = lax.all_to_all(sent, PLANE, split_axis=0, concat_axis=0, tiled=True)  25.8 us
    all_to_all x1, waiting for transfers between devices, per_device(): mine = lax.all_to_all(enter, PLANE, split_axis=0, concat_axis=0, tiled=True)  24.4 us
    all_to_all x1, starting transfers between devices, per_device(): got = lax.all_to_all(sent, PLANE, split_axis=0, concat_axis=0, tiled=True)  18.4 us
    all_to_all x1, waiting for transfers between devices, per_device(): totals = lax.all_to_all(total, 'z', split_axis=0, concat_axis=0, tiled=True)  13.8 us
    pallas_call x3, Pallas kernels, per_device(): call(functools.partial(within, heads=mine), (shape((tokens, len(mine) * E...  12.5 us
    all_to_all x1, starting transfers between devices, per_device(): totals = lax.all_to_all(total, 'z', split_axis=0, concat_axis=0, tiled=True)  11.9 us
    all_to_all x1, starting transfers between devices, per_device(): mine = lax.all_to_all(enter, PLANE, split_axis=0, concat_axis=0, tiled=True)  8.87 us
    pallas_call x1, Pallas kernels, per_device(): call(finish, shape((tokens, heads * E), BF16), [SMEM, SMEM] + [VMEM] * (4...  5.87 us
  transfers between devices with their start and end apart: 3, of which 3 were waited for; matrix products, arithmetic and copies ran while one was open for 0% of the time, Pallas kernels for 9%

profile of v1, /device:TPU:1, one launch (start us, length us, event | category | flops | bytes accessed | tf_op | source)
XLA Modules:
  0.0 134.4 jit_solution(4816256192027085245)
XLA Ops:
  0.0 1.4 %copy.11.decay_ref = bf16[96,32]{1,0:T(8,128)(2,1)} copy(bf16[96,32]{0,1:T(8,128)(2,1)} %param.9) | data formatting | bytes 12288 | tf_op args[3]
  1.4 3.7 %summarize.1 = bf16[64,72,128]{2,1,0:T(8,128)(2,1)} custom-call(s32[1]{0:T(128)} %bitcast.first_ref, s32[9]{0:T(128)} %starts_ref.9, bf16[96,4096]{1,0:T(8,128)(2,1)} %k_ref.7, bf16[96,4096]{1,0:T(8,128)(2,1)} %v_ref.7, bf16[96,32]{1,0:T(8,128)(2,1)} %copy.11.decay_ref, f32[1,128]{1,0:T(1,128)} %bitcast.3), custom_call_target="tpu_custom_call" | custom-call | flops 100663296 | bytes 2359296 | tf_op jit(solution)/shard_map/summarize/pallas_call | solution.py:177
  5.1 18.4 %all-to-all-start = ((bf16[64,72,128]{2,1,0:T(8,128)(2,1)}), bf16[64,72,128]{2,1,0:T(8,128)(2,1)S(1)}, u32[]{:S(2)}, u32[]{:S(2)}) async-start(bf16[64,72,128]{2,1,0:T(8,128)(2,1)} %summarize.1), calls=%async_computation | async-start | bytes 2359296 | tf_op jit(solution)/shard_map/all_to_all | solution.py:181
  23.5 5.0 %within0.1 = (f32[96,2048]{1,0:T(8,128)}, f32[8,128]{1,0:T(8,128)}) custom-call(s32[1]{0:T(128)} %bitcast.first_ref, s32[9]{0:T(128)} %starts_ref.9, bf16[96,4096]{1,0:T(8,128)(2,1)} %q_ref.7, bf16[96,4096]{1,0:T(8,128)(2,1)} %k_ref.7, bf16[96,4096]{1,0:T(8,128)(2,1)} %v_ref.7, bf16[96,32]{1,0:T(8,128)(2,1)} %copy.11.decay_ref), custom_call_target="tpu_custom_call" | custom-call | flops 75497472 | bytes 1966080 | tf_op jit(solution)/shard_map/within0/pallas_call | solution.py:185
  28.6 25.8 %all-to-all-done.got_ref = bf16[64,72,128]{2,1,0:T(8,128)(2,1)S(1)} async-done(((bf16[64,72,128]{2,1,0:T(8,128)(2,1)}), bf16[64,72,128]{2,1,0:T(8,128)(2,1)S(1)}, u32[]{:S(2)}, u32[]{:S(2)}) %all-to-all-start) | async-done | bytes 1179680 | tf_op jit(solution)/shard_map/all_to_all | solution.py:181
  54.3 0.0 copy-start
  54.3 1.0 copy-done
  55.3 2.3 %plane_total.1 = (bf16[16,72,128]{2,1,0:T(8,128)(2,1)}, f32[32,128]{1,0:T(8,128)}) custom-call(bf16[64,72,128]{2,1,0:T(8,128)(2,1)} %copy-done, f32[8,128]{1,0:T(8,128)} %get-tuple-element.15._), custom_call_target="tpu_custom_call" | custom-call | flops 2097152 | bytes 1179648 | tf_op jit(solution)/shard_map/plane_total/pallas_call | solution.py:192
  57.6 11.9 %all-to-all-start.1 = ((bf16[16,72,128]{2,1,0:T(8,128)(2,1)}), bf16[16,72,128]{2,1,0:T(8,128)(2,1)S(1)}, u32[]{:S(2)}, u32[]{:S(2)}) async-start(bf16[16,72,128]{2,1,0:T(8,128)(2,1)} %get-tuple-element.16), calls=%async_computation.1 | async-start | bytes 589824 | tf_op jit(solution)/shard_map/all_to_all | solution.py:196
  69.5 3.7 %within1.1 = (f32[96,1024]{1,0:T(8,128)}, f32[8,128]{1,0:T(8,128)}) custom-call(s32[1]{0:T(128)} %bitcast.first_ref, s32[9]{0:T(128)} %starts_ref.9, bf16[96,4096]{1,0:T(8,128)(2,1)} %q_ref.7, bf16[96,4096]{1,0:T(8,128)(2,1)} %k_ref.7, bf16[96,4096]{1,0:T(8,128)(2,1)} %v_ref.7, bf16[96,32]{1,0:T(8,128)(2,1)} %copy.11.decay_ref), custom_call_target="tpu_custom_call" | custom-call | flops 37748736 | bytes 983040 | tf_op jit(solution)/shard_map/within1/pallas_call | solution.py:185
  73.3 13.8 %all-to-all-done.1.planes_ref = bf16[16,72,128]{2,1,0:T(8,128)(2,1)S(1)} async-done(((bf16[16,72,128]{2,1,0:T(8,128)(2,1)}), bf16[16,72,128]{2,1,0:T(8,128)(2,1)S(1)}, u32[]{:S(2)}, u32[]{:S(2)}) %all-to-all-start.1) | async-done | bytes 294944 | tf_op jit(solution)/shard_map/all_to_all | solution.py:196
  87.1 0.0 copy-start.2
  87.1 0.7 copy-done.2
  87.8 2.7 %entering.1 = bf16[64,64,128]{2,1,0:T(8,128)(2,1)} custom-call(s32[1]{0:T(128)} %bitcast.1.plane_ref, bf16[16,72,128]{2,1,0:T(8,128)(2,1)} %copy-done.2, bf16[64,72,128]{2,1,0:T(8,128)(2,1)} %copy-done, f32[8,128]{1,0:T(8,128)} %get-tuple-element.17._), custom_call_target="tpu_custom_call" | custom-call | flops 2097152 | bytes 2097152 | tf_op jit(solution)/shard_map/entering/pallas_call | solution.py:197
  90.5 8.9 %all-to-all-start.2 = ((bf16[64,64,128]{2,1,0:T(8,128)(2,1)}), bf16[64,64,128]{2,1,0:T(8,128)(2,1)S(1)}, u32[]{:S(2)}, u32[]{:S(2)}) async-start(bf16[64,64,128]{2,1,0:T(8,128)(2,1)} %entering.1), calls=%async_computation.2 | async-start | bytes 2097152 | tf_op jit(solution)/shard_map/all_to_all | solution.py:201
  99.4 3.7 %within2.1 = (f32[96,1024]{1,0:T(8,128)}, f32[8,128]{1,0:T(8,128)}) custom-call(s32[1]{0:T(128)} %bitcast.first_ref, s32[9]{0:T(128)} %starts_ref.9, bf16[96,4096]{1,0:T(8,128)(2,1)} %q_ref.7, bf16[96,4096]{1,0:T(8,128)(2,1)} %k_ref.7, bf16[96,4096]{1,0:T(8,128)(2,1)} %v_ref.7, bf16[96,32]{1,0:T(8,128)(2,1)} %copy.11.decay_ref), custom_call_target="tpu_custom_call" | custom-call | flops 37748736 | bytes 983040 | tf_op jit(solution)/shard_map/within2/pallas_call | solution.py:185
  103.1 24.4 %all-to-all-done.2.refs_3_ = bf16[64,64,128]{2,1,0:T(8,128)(2,1)S(1)} async-done(((bf16[64,64,128]{2,1,0:T(8,128)(2,1)}), bf16[64,64,128]{2,1,0:T(8,128)(2,1)S(1)}, u32[]{:S(2)}, u32[]{:S(2)}) %all-to-all-start.2) | async-done | bytes 1048608 | tf_op jit(solution)/shard_map/all_to_all | solution.py:201
  127.5 0.0 copy-start.1
  127.5 1.0 copy-done.1
  128.5 5.9 %finish.1 = bf16[96,4096]{1,0:T(8,128)(2,1)} custom-call(s32[1]{0:T(128)} %bitcast.first_ref, s32[9]{0:T(128)} %starts_ref.9, bf16[96,4096]{1,0:T(8,128)(2,1)} %q_ref.7, bf16[96,32]{1,0:T(8,128)(2,1)} %copy.11.decay_ref, f32[96,2048]{1,0:T(8,128)} %get-tuple-element.12.refs_0_, f32[96,1024]{1,0:T(8,128)} %get-tuple-element.13.refs_1_, ...), custom_call_target="tpu_custom_call" | custom-call | flops 100663296 | bytes 3932160 | tf_op jit(solution)/shard_map/finish/pallas_call | solution.py:202
Async XLA Ops:
  5.1 49.2 %all-to-all-start = ((bf16[64,72,128]{2,1,0:T(8,128)(2,1)}), bf16[64,72,128]{2,1,0:T(8,128)(2,1)S(1)}, u32[]{:S(2)}, u32[]{:S(2)}) async-start(bf16[64,72,128]{2,1,0:T(8,128)(2,1)} %summarize.1), calls=%async_computation | async-start | bytes 2359296 | tf_op jit(solution)/shard_map/all_to_all | solution.py:181
  54.3 1.0 copy-start
  57.6 29.5 %all-to-all-start.1 = ((bf16[16,72,128]{2,1,0:T(8,128)(2,1)}), bf16[16,72,128]{2,1,0:T(8,128)(2,1)S(1)}, u32[]{:S(2)}, u32[]{:S(2)}) async-start(bf16[16,72,128]{2,1,0:T(8,128)(2,1)} %get-tuple-element.16), calls=%async_computation.1 | async-start | bytes 589824 | tf_op jit(solution)/shard_map/all_to_all | solution.py:196
  87.1 0.7 copy-start.2
  90.5 37.0 %all-to-all-start.2 = ((bf16[64,64,128]{2,1,0:T(8,128)(2,1)}), bf16[64,64,128]{2,1,0:T(8,128)(2,1)S(1)}, u32[]{:S(2)}, u32[]{:S(2)}) async-start(bf16[64,64,128]{2,1,0:T(8,128)(2,1)} %entering.1), calls=%async_computation.2 | async-start | bytes 2097152 | tf_op jit(solution)/shard_map/all_to_all | solution.py:201
  127.5 1.0 copy-start.1

commit v2 on v1

v2 whole, which is shorter than its diff:
```python
import functools

import jax
import jax.numpy as jnp
from jax import lax
from jax.experimental import pallas as pl
from jax.experimental.pallas import tpu as pltpu
from jax.sharding import Mesh, PartitionSpec as P

E = 128
HALF = E // 2
QUARTER = E // 4
NX = 4
AXES = ("zh", "zl", "core", "y", "x")
NEAR = ("core", "x")
MIDDLE = ("zl", "y")
FAR = "zh"
F32, BF16 = jnp.float32, jnp.bfloat16
SMALL = 14 << 20
VMEM = pl.BlockSpec(memory_space=pltpu.VMEM)
SMEM = pl.BlockSpec(memory_space=pltpu.SMEM)
HBM = pl.BlockSpec(memory_space=pltpu.HBM)


def started(position, starts_ref):
    count = jnp.zeros_like(position)
    for i in range(starts_ref.shape[0] - 1):
        count = count + (position >= starts_ref[i]).astype(jnp.int32)
    return count


def cumulative(decay_ref):
    tokens = decay_ref.shape[1]
    i = lax.broadcasted_iota(jnp.int32, (tokens, tokens), 0)
    j = lax.broadcasted_iota(jnp.int32, (tokens, tokens), 1)
    lower = (i >= j).astype(BF16)
    return lax.dot_general(lower, decay_ref[...], (((1,), (1,)), ((), ())), preferred_element_type=F32)


def parts(value):
    high = value.astype(BF16).astype(F32)
    return high, (value - high).astype(BF16).astype(F32)


def rows_of(values, count):
    row = lax.broadcasted_iota(jnp.int32, (count, E), 0)
    tile = jnp.zeros((count, E), F32)
    for n, value in enumerate(values):
        for i, part in enumerate(parts(value)):
            tile = jnp.where(row == 2 * n + i, jnp.broadcast_to(part, (count, E)), tile)
    return tile.astype(BF16)


def value_of(tile, n):
    return tile[2 * n : 2 * n + 1] + tile[2 * n + 1 : 2 * n + 2]


def column(h):
    return slice(h * E, (h + 1) * E)


def summarize(first_ref, starts_ref, k_ref, v_ref, decay_ref, out_ref, piece_ref, sems):
    heads, tokens = decay_ref.shape
    each = heads // NX
    first = first_ref[0]
    position = first + lax.broadcasted_iota(jnp.int32, (tokens, 1), 0)
    at_end = started(first + tokens - 1, starts_ref)
    cum = cumulative(decay_ref)
    last = cum[tokens - 1 :, :]
    tail = jnp.where(started(position, starts_ref) == at_end, jnp.exp(last - cum), 0.0)
    open_all = at_end == started(first - 1, starts_ref)
    keep = jnp.where(open_all, jnp.exp(last), 0.0)
    copies = []
    for x in range(NX):
        mine = [n * NX + x for n in range(each)]
        for n, h in enumerate(mine):
            scaled = (k_ref[:, column(h)].astype(F32) * tail[:, h : h + 1]).astype(BF16)
            state = lax.dot_general(
                scaled, v_ref[:, column(h)], (((0,), (0,)), ((), ())), preferred_element_type=F32
            ).astype(BF16)
            for c in range(2):
                piece_ref[c * NX + x, n * HALF : (n + 1) * HALF, :] = state[c * HALF : (c + 1) * HALF]
        extra = rows_of([keep[:, h : h + 1] for h in mine], 2 * each)
        for c in range(2):
            p = c * NX + x
            piece_ref[p, each * HALF :, :] = extra
            copies.append(pltpu.make_async_copy(piece_ref.at[p], out_ref.at[p], sems.at[p]))
            copies[-1].start()
    for copy in copies:
        copy.wait()


def within(first_ref, starts_ref, q_ref, k_ref, v_ref, decay_ref, out_ref, done_ref, *, heads):
    done_ref[...] = jnp.zeros_like(done_ref)
    tokens = decay_ref.shape[1]
    first = first_ref[0]
    i = lax.broadcasted_iota(jnp.int32, (tokens, tokens), 0)
    j = lax.broadcasted_iota(jnp.int32, (tokens, tokens), 1)
    mask = (i >= j) & (started(first + i, starts_ref) == started(first + j, starts_ref))
    cum = cumulative(decay_ref)
    across = cum.T
    for n, h in enumerate(heads):
        scores = lax.dot_general(
            q_ref[:, column(n)], k_ref[:, column(n)], (((1,), (1,)), ((), ())), preferred_element_type=F32
        )
        decay = jnp.exp(jnp.where(mask, cum[:, h : h + 1] - across[h : h + 1, :], -1e30))
        weights = (scores * decay).astype(BF16)
        out_ref[:, column(n)] = jnp.dot(weights, v_ref[:, column(n)], preferred_element_type=F32)


def row_total(near_ref, _, out_ref):
    sources, rows = near_ref.shape[0], near_ref.shape[1]
    each = rows // (HALF + 2)
    keeps = [near_ref[p, each * HALF :, :].astype(F32) for p in range(sources)]
    for n in range(each):
        totals = []
        for c in range(2):
            state = near_ref[c * NX, n * HALF : (n + 1) * HALF, :].astype(F32)
            total = value_of(keeps[c * NX], n)
            for x in range(1, NX):
                mine = value_of(keeps[c * NX + x], n)
                state = mine * state + near_ref[c * NX + x, n * HALF : (n + 1) * HALF, :].astype(F32)
                total = mine * total
            for z in range(2):
                out_ref[z * each + n, c * QUARTER : (c + 1) * QUARTER, :] = state[
                    z * QUARTER : (z + 1) * QUARTER
                ].astype(BF16)
            totals.append(total)
        extra = rows_of(totals, 8)
        for z in range(2):
            out_ref[z * each + n, HALF:, :] = extra


def in_order(sources):
    each = sources // 2
    return [(z * each + y, c) for z in range(2) for c in range(2) for y in range(each)]


def block_total(middle_ref, out_ref):
    state, total = jnp.zeros((QUARTER, E), F32), jnp.ones((1, E), F32)
    for p, c in in_order(middle_ref.shape[0]):
        mine = value_of(middle_ref[p, HALF:, :].astype(F32), c)
        state = mine * state + middle_ref[p, c * QUARTER : (c + 1) * QUARTER, :].astype(F32)
        total = mine * total
    state, extra = state.astype(BF16), rows_of([total], 8)
    for z in range(out_ref.shape[0]):
        out_ref[z, 0:QUARTER, :] = state
        out_ref[z, QUARTER:, :] = extra


def enter_rows(block_ref, far_ref, middle_ref, gain_ref, out_ref):
    def earlier(n, state):
        keep = value_of(far_ref[n, QUARTER:, :].astype(F32), 0)
        return keep * state + far_ref[n, 0:QUARTER, :].astype(F32)

    state = lax.fori_loop(0, block_ref[0], earlier, jnp.zeros((QUARTER, E), F32))
    for p, c in in_order(middle_ref.shape[0]):
        out_ref[p, c * QUARTER : (c + 1) * QUARTER, :] = state.astype(BF16)
        mine = value_of(middle_ref[p, HALF:, :].astype(F32), c)
        state = mine * state + middle_ref[p, c * QUARTER : (c + 1) * QUARTER, :].astype(F32)
    extra = rows_of([gain_ref[...]], 8)
    for p in range(out_ref.shape[0]):
        out_ref[p, HALF:, :] = extra


def enter_chunks(middle_ref, near_ref, out_ref, piece_ref, state_ref, sems):
    sources, rows = near_ref.shape[0], near_ref.shape[1]
    each = rows // (HALF + 2)
    gains = [middle_ref[n, HALF:, :] for n in range(each)]
    copies = []
    for c in range(2):
        for x in range(NX):
            p = c * NX + x
            keeps = near_ref[p, each * HALF :, :].astype(F32)
            for n in range(each):
                if x == 0:
                    state = jnp.concatenate(
                        [
                            middle_ref[z * each + n, c * QUARTER : (c + 1) * QUARTER, :].astype(F32)
                            for z in range(2)
                        ]
                    )
                else:
                    state = state_ref[n]
                piece_ref[p, n * HALF : (n + 1) * HALF, :] = state.astype(BF16)
                piece_ref[p, each * HALF + 2 * n : each * HALF + 2 * n + 2, :] = gains[n][0:2]
                if x < NX - 1:
                    state_ref[n] = value_of(keeps, n) * state + near_ref[
                        p, n * HALF : (n + 1) * HALF, :
                    ].astype(F32)
            copies.append(pltpu.make_async_copy(piece_ref.at[p], out_ref.at[p], sems.at[p]))
            copies[-1].start()
    for copy in copies:
        copy.wait()


def finish(first_ref, starts_ref, q_ref, decay_ref, *refs):
    early_ref, late_hbm, enter_ref, out_ref, late_ref, sem = refs
    late = pltpu.make_async_copy(late_hbm, late_ref, sem)
    late.start()
    heads, tokens = decay_ref.shape
    each = heads // NX
    first = first_ref[0]
    position = first + lax.broadcasted_iota(jnp.int32, (tokens, 1), 0)
    opened = started(position, starts_ref) == started(first - 1, starts_ref)
    reach = jnp.where(opened, jnp.exp(cumulative(decay_ref)), 0.0)
    places = [(ref, n) for ref in (early_ref, late_ref) for n in range(ref.shape[1] // E)]
    gains = [enter_ref[x, each * HALF :, :].astype(F32) for x in range(NX)]
    for h in range(heads):
        ref, m = places[h]
        if ref is late_ref and m == 0:
            late.wait()
        n, x = divmod(h, NX)
        state = jnp.concatenate([enter_ref[c * NX + x, n * HALF : (n + 1) * HALF, :] for c in range(2)], axis=0)
        inter = jnp.dot(q_ref[:, column(h)], state, preferred_element_type=F32)
        attn = ref[:, column(m)] + inter * reach[:, h : h + 1]
        meansq = jnp.mean(attn * attn, axis=-1, keepdims=True)
        normed = attn * lax.rsqrt(meansq + 1e-05) * value_of(gains[x], n)
        out_ref[:, column(h)] = normed.astype(BF16)


def call(kernel, out, specs, name, flops, nbytes, limit=None, out_specs=None, scratch=(), grid=()):
    return pl.pallas_call(
        kernel,
        out_shape=out,
        grid=grid,
        in_specs=specs,
        out_specs=jax.tree.map(lambda _: VMEM, out) if out_specs is None else out_specs,
        scratch_shapes=scratch,
        name=name,
        compiler_params=pltpu.CompilerParams(vmem_limit_bytes=limit),
        cost_estimate=pl.CostEstimate(flops=flops, bytes_accessed=nbytes, transcendentals=0),
    )


def exchange(value, axes):
    return lax.all_to_all(value, axes, split_axis=0, concat_axis=0, tiled=True)


def per_device(queries, keys, values, log_decay, gain, doc_starts):
    tokens, heads = log_decay.shape
    each = heads // NX
    far = lax.axis_size(FAR)
    first = (lax.axis_index(AXES) * tokens).astype(jnp.int32).reshape(1)
    block = lax.axis_index(FAR).astype(jnp.int32).reshape(1)
    decay = log_decay.T
    shape = jax.ShapeDtypeStruct
    tri = 2 * tokens * tokens * E
    square = 2 * tokens * E * E
    near_shape = (2 * NX, each * (HALF + 2), E)
    middle_shape = (2 * each, HALF + 8, E)
    near_scratch = pltpu.VMEM(near_shape, BF16)
    near_bytes = 2 * 2 * heads * HALF * E

    sent = call(
        summarize, shape(near_shape, BF16), [SMEM, SMEM, VMEM, VMEM, VMEM], "summarize",
        heads * square, 4 * tokens * heads * E + near_bytes, out_specs=HBM,
        scratch=[near_scratch, pltpu.SemaphoreType.DMA((2 * NX,))],
    )(first, doc_starts, keys, values, decay)
    near = exchange(sent, NEAR)

    inside, done = [], []
    share = heads // 2
    for s in range(2):
        mine = tuple(range(s * share, (s + 1) * share))
        part = pl.BlockSpec((tokens, share * E), functools.partial(lambda s, i: (0, s), s))
        attn, after = call(
            functools.partial(within, heads=mine), (shape((tokens, share * E), F32), shape((8, E), F32)),
            [SMEM, SMEM, part, part, part, pl.BlockSpec((heads, tokens), lambda i: (0, 0))], f"within{s}",
            2 * share * tri, 10 * tokens * share * E, grid=(1,),
            out_specs=(pl.BlockSpec((tokens, share * E), lambda i: (0, 0)), pl.BlockSpec((8, E), lambda i: (0, 0))),
        )(first, doc_starts, queries, keys, values, decay)
        inside.append(attn)
        done.append(after)

    rows = call(
        row_total, shape(middle_shape, BF16), [VMEM, HBM], "row_total", 2 * near_bytes, near_bytes, SMALL,
    )(near, done[0])
    middle = exchange(rows, MIDDLE)
    total = call(
        block_total, shape((far, QUARTER + 8, E), BF16), [VMEM], "block_total", near_bytes, near_bytes // 4, SMALL,
    )(middle)
    totals = exchange(total, FAR)
    row_states = call(
        enter_rows, shape(middle_shape, BF16), [SMEM, VMEM, VMEM, VMEM], "enter_rows", near_bytes, near_bytes // 2, SMALL,
    )(block, totals, middle, gain.reshape(1, E))
    row_states = exchange(row_states, MIDDLE)
    states = call(
        enter_chunks, shape(near_shape, BF16), [VMEM, VMEM], "enter_chunks", 2 * near_bytes, 2 * near_bytes, SMALL,
        out_specs=HBM,
        scratch=[near_scratch, pltpu.VMEM((each, HALF, E), F32), pltpu.SemaphoreType.DMA((2 * NX,))],
    )(row_states, near)
    states = exchange(states, NEAR)
    return call(
        finish, shape((tokens, heads * E), BF16), [SMEM, SMEM, VMEM, VMEM, VMEM, HBM, VMEM], "finish",
        heads * square, 10 * tokens * heads * E, SMALL,
        scratch=[pltpu.VMEM((tokens, share * E), F32), pltpu.SemaphoreType.DMA],
    )(first, doc_starts, queries, decay, *inside, states)


def solution(mesh):
    ctx, heads = mesh.devices.shape
    split = Mesh(mesh.devices.reshape(ctx // 4, 2, 2, heads // NX, NX), AXES)
    rows = P(AXES, None)
    return jax.shard_map(
        per_device,
        mesh=split,
        in_specs=(rows, rows, rows, rows, P(("y", "x")), P()),
        out_specs=rows,
        check_vma=False,
    )
```

time: 135 us -> 117 us (0.87)
  blocking collectives: 0 us -> 49.7 us
  waiting for transfers between devices: 64 us -> 21.2 us
  starting transfers between devices: 39.2 us -> 24.8 us
  Pallas kernels: 27 us -> 18.7 us
  local copies, waits for them, and re-layouts: 4.12 us -> 1.83 us
    all_to_all x0 -> x3, blocking collectives: none -> 49.7 us  [exchange(): return lax.all_to_all(value, axes, split_axis=0, concat_axis=0, tiled=True)]
    all_to_all x3 -> x2, waiting for transfers between devices: 64 us -> 21.2 us  [exchange(): return lax.all_to_all(value, axes, split_axis=0, concat_axis=0, tiled=True)]
    all_to_all x3 -> x2, starting transfers between devices: 39.2 us -> 24.8 us  [exchange(): return lax.all_to_all(value, axes, split_axis=0, concat_axis=0, tiled=True)]
    pallas_call x7 -> x8, Pallas kernels: 27 us -> 18.7 us  [the longest x2 9.42 us: per_device(): call(functools.partial(within, heads=mine), (shape((tokens, share * E), F...]
    unnamed x7 -> x14, local copies, waits for them, and re-layouts: 4.12 us -> 1.83 us
  transfers between devices with their start and end apart: 3 -> 2, of which waited for: 3 -> 2; matrix products, arithmetic and copies ran while one was open for 0% -> 0% of each run, Pallas kernels for 9% -> 8%
where the time goes in v2:
time: 117 us; the launch traced here: 116 us
  blocking collectives  49.7 us (42%)
  starting transfers between devices  24.8 us (21%)
  waiting for transfers between devices  21.2 us (18%)
  Pallas kernels  18.7 us (16%)
  local copies, waits for them, and re-layouts  1.83 us (2%)
    all_to_all x3, blocking collectives, exchange(): return lax.all_to_all(value, axes, split_axis=0, concat_axis=0, tiled=True)  49.7 us
    all_to_all x2, starting transfers between devices, exchange(): return lax.all_to_all(value, axes, split_axis=0, concat_axis=0, tiled=True)  24.8 us
    all_to_all x2, waiting for transfers between devices, exchange(): return lax.all_to_all(value, axes, split_axis=0, concat_axis=0, tiled=True)  21.2 us
    pallas_call x2, Pallas kernels, per_device(): call(functools.partial(within, heads=mine), (shape((tokens, share * E), F...  9.42 us
    pallas_call x1, Pallas kernels, per_device(): call(finish, shape((tokens, heads * E), BF16), [SMEM, SMEM, VMEM, VMEM, V...  4.44 us
    pallas_call x1, Pallas kernels, per_device(): call(summarize, shape(near_shape, BF16), [SMEM, SMEM, VMEM, VMEM, VMEM],...  3.38 us
  transfers between devices with their start and end apart: 2, of which 2 were waited for; matrix products, arithmetic and copies ran while one was open for 0% of the time, Pallas kernels for 8%

profile of v2, /device:TPU:1, one launch (start us, length us, event | category | flops | bytes accessed | tf_op | source)
XLA Modules:
  0.0 116.3 jit_solution(10170447849902337733)
XLA Ops:
  0.0 3.4 %summarize.1 = bf16[8,528,128]{2,1,0:T(8,128)(2,1)} custom-call(s32[1]{0:T(128)} %bitcast.first_ref, s32[9]{0:T(128)} %starts_ref.7, bf16[96,4096]{1,0:T(8,128)(2,1)} %k_ref.5, bf16[96,4096]{1,0:T(8,128)(2,1)} %v_ref.5, bf16[32,96]{1,0:T(8,128)(2,1)} %bitcast.4), custom_call_target="tpu_custom_call" | custom-call | flops 100663296 | bytes 2621440 | tf_op jit(solution)/shard_map/summarize/pallas_call | solution.py:255
  3.4 17.6 %all-to-all-start = ((bf16[8,528,128]{2,1,0:T(8,128)(2,1)}), bf16[8,528,128]{2,1,0:T(8,128)(2,1)S(1)}, u32[]{:S(2)}, u32[]{:S(2)}) async-start(bf16[8,528,128]{2,1,0:T(8,128)(2,1)} %summarize.1), calls=%async_computation | async-start | bytes 2162688 | tf_op jit(solution)/shard_map/all_to_all | solution.py:237
  21.0 4.6 %within0.1 = (f32[96,2048]{1,0:T(8,128)}, f32[8,128]{1,0:T(8,128)}) custom-call(s32[1]{0:T(128)} %bitcast.first_ref, s32[9]{0:T(128)} %starts_ref.7, bf16[96,4096]{1,0:T(8,128)(2,1)} %q_ref.5, bf16[96,4096]{1,0:T(8,128)(2,1)} %k_ref.5, bf16[96,4096]{1,0:T(8,128)(2,1)} %v_ref.5, bf16[32,96]{1,0:T(8,128)(2,1)} %bitcast.5), custom_call_target="tpu_custom_call" | custom-call | flops 75497472 | bytes 1966080 | tf_op jit(solution)/shard_map/within0/pallas_call | solution.py:267
  25.6 10.7 %all-to-all-done.near_ref = bf16[8,528,128]{2,1,0:T(8,128)(2,1)S(1)} async-done(((bf16[8,528,128]{2,1,0:T(8,128)(2,1)}), bf16[8,528,128]{2,1,0:T(8,128)(2,1)S(1)}, u32[]{:S(2)}, u32[]{:S(2)}) %all-to-all-start) | async-done | bytes 1081376 | tf_op jit(solution)/shard_map/all_to_all | solution.py:237
  36.3 0.0 copy-start.5
  36.3 0.7 copy-done.5
  37.0 0.0 copy-start.6
  37.0 0.2 row_total.1
  37.2 11.4 %all_to_all.25.middle_ref = bf16[16,72,128]{2,1,0:T(8,128)(2,1)S(1)} all-to-all(bf16[16,72,128]{2,1,0:T(8,128)(2,1)S(1)} %row_total.1), channel_id=1, replica_groups=mesh['zh'=8,'zl'=2,'core'=2,'y'=8,'x'=4] {'zl','y'}, dimensions={0} | all-to-all | bytes 589824 | tf_op jit(solution)/shard_map/all_to_all | solution.py:237
  48.6 0.1 block_total.1
  48.7 23.8 %all_to_all.26.far_ref = bf16[8,40,128]{2,1,0:T(8,128)(2,1)S(1)} all-to-all(bf16[8,40,128]{2,1,0:T(8,128)(2,1)S(1)} %block_total.1), channel_id=1, replica_groups=mesh['zh'=8,'zl'=2,'core'=2,'y'=8,'x'=4] {'zh'}, dimensions={0} | all-to-all | bytes 163840 | tf_op jit(solution)/shard_map/all_to_all | solution.py:237
  72.5 0.0 copy-done.6
  72.5 0.1 enter_rows.1
  72.6 14.5 %all_to_all.27.middle_ref = bf16[16,72,128]{2,1,0:T(8,128)(2,1)S(1)} all-to-all(bf16[16,72,128]{2,1,0:T(8,128)(2,1)S(1)} %enter_rows.1), channel_id=1, replica_groups=mesh['zh'=8,'zl'=2,'core'=2,'y'=8,'x'=4] {'zl','y'}, dimensions={0} | all-to-all | bytes 589824 | tf_op jit(solution)/shard_map/all_to_all | solution.py:237
  87.1 1.1 enter_chunks.1
  88.2 7.2 %all-to-all-start.4 = ((bf16[8,528,128]{2,1,0:T(8,128)(2,1)}), bf16[8,528,128]{2,1,0:T(8,128)(2,1)S(1)}, u32[]{:S(2)}, u32[]{:S(2)}) async-start(bf16[8,528,128]{2,1,0:T(8,128)(2,1)} %enter_chunks.1), calls=%async_computation.4 | async-start | bytes 2162688 | tf_op jit(solution)/shard_map/all_to_all | solution.py:237
  95.4 0.0 copy-start
  95.4 0.0 copy-start.1
  95.4 0.0 copy-start.3
  95.4 0.0 copy-start.4
  95.4 4.8 %within1.1 = (f32[96,2048]{1,0:T(8,128)}, f32[8,128]{1,0:T(8,128)}) custom-call(s32[1]{0:T(128)} %bitcast.first_ref, s32[9]{0:T(128)} %starts_ref.7, bf16[96,4096]{1,0:T(8,128)(2,1)} %q_ref.5, bf16[96,4096]{1,0:T(8,128)(2,1)} %k_ref.5, bf16[96,4096]{1,0:T(8,128)(2,1)} %v_ref.5, bf16[32,96]{1,0:T(8,128)(2,1)} %bitcast.6), custom_call_target="tpu_custom_call" | custom-call | flops 75497472 | bytes 1966080 | tf_op jit(solution)/shard_map/within1/pallas_call | solution.py:267
  100.2 10.5 %all-to-all-done.4.refs_2_ = bf16[8,528,128]{2,1,0:T(8,128)(2,1)S(1)} async-done(((bf16[8,528,128]{2,1,0:T(8,128)(2,1)}), bf16[8,528,128]{2,1,0:T(8,128)(2,1)S(1)}, u32[]{:S(2)}, u32[]{:S(2)}) %all-to-all-start.4) | async-done | bytes 1081376 | tf_op jit(solution)/shard_map/all_to_all | solution.py:237
  110.7 0.0 copy-done
  110.7 0.0 copy-done.1
  110.7 0.0 copy-done.3
  110.7 0.0 copy-done.4
  110.7 0.0 copy-start.2
  110.7 1.1 copy-done.2
  111.8 4.4 %finish.1 = bf16[96,4096]{1,0:T(8,128)(2,1)} custom-call(s32[1]{0:T(128)} %bitcast.first_ref, s32[9]{0:T(128)S(1)} %copy-done.4, bf16[96,4096]{1,0:T(8,128)(2,1)S(1)} %copy-done, bf16[32,96]{1,0:T(8,128)(2,1)S(1)} %bitcast.7, f32[96,2048]{1,0:T(8,128)S(1)} %copy-done.1, f32[96,2048]{1,0:T(8,128)S(1)} %copy-done.2, ...), custom_call_target="tpu_custom_call" | custom-call | flops 100663296 | bytes 3932160 | tf_op jit(solution)/shard_map/finish/pallas_call | solution.py:294
Async XLA Ops:
  3.4 32.9 %all-to-all-start = ((bf16[8,528,128]{2,1,0:T(8,128)(2,1)}), bf16[8,528,128]{2,1,0:T(8,128)(2,1)S(1)}, u32[]{:S(2)}, u32[]{:S(2)}) async-start(bf16[8,528,128]{2,1,0:T(8,128)(2,1)} %summarize.1), calls=%async_computation | async-start | bytes 2162688 | tf_op jit(solution)/shard_map/all_to_all | solution.py:237
  36.3 0.7 copy-start.5
  37.0 35.5 %copy-start.6 = (f32[128]{0:T(128)S(1)}, f32[128]{0:T(128)}, u32[]{:S(2)}) copy-start(f32[128]{0:T(128)} %param.10) | copy-start | bytes 1540
  88.2 22.5 %all-to-all-start.4 = ((bf16[8,528,128]{2,1,0:T(8,128)(2,1)}), bf16[8,528,128]{2,1,0:T(8,128)(2,1)S(1)}, u32[]{:S(2)}, u32[]{:S(2)}) async-start(bf16[8,528,128]{2,1,0:T(8,128)(2,1)} %enter_chunks.1), calls=%async_computation.4 | async-start | bytes 2162688 | tf_op jit(solution)/shard_map/all_to_all | solution.py:237
  95.4 15.3 %copy-start = (bf16[96,4096]{1,0:T(8,128)(2,1)S(1)}, bf16[96,4096]{1,0:T(8,128)(2,1)}, u32[]{:S(2)}) copy-start(bf16[96,4096]{1,0:T(8,128)(2,1)} %q_ref.5) | copy-start | bytes 2359300
  95.4 15.3 %copy-start.1 = (f32[96,2048]{1,0:T(8,128)S(1)}, f32[96,2048]{1,0:T(8,128)}, u32[]{:S(2)}) copy-start(f32[96,2048]{1,0:T(8,128)} %get-tuple-element.8.refs_0_) | copy-start | bytes 2359300
  95.4 15.3 %copy-start.3 = (bf16[96,32]{0,1:T(8,128)(2,1)S(1)}, bf16[96,32]{0,1:T(8,128)(2,1)}, u32[]{:S(2)}) copy-start(bf16[96,32]{0,1:T(8,128)(2,1)} %param.9) | copy-start | bytes 18436
  95.4 15.3 %copy-start.4 = (s32[9]{0:T(128)S(1)}, s32[9]{0:T(128)}, u32[]{:S(2)}) copy-start(s32[9]{0:T(128)} %starts_ref.7) | copy-start | bytes 112
  110.7 1.1 copy-start.2

commit v3 on v2

v3 whole, which is shorter than its diff:
```python
import jax
import jax.numpy as jnp
from jax import lax
from jax.experimental import pallas as pl
from jax.experimental.pallas import tpu as pltpu
from jax.sharding import Mesh, PartitionSpec as P

E = 128
HALF = E // 2
QUARTER = E // 4
NS = 8
AXES = ("zh", "zl", "core", "yh", "yl", "x")
NEAR = ("core", "yl", "x")
MIDDLE = ("zl", "yh")
FAR = "zh"
F32, BF16 = jnp.float32, jnp.bfloat16
SMALL = 14 << 20
VMEM = pl.BlockSpec(memory_space=pltpu.VMEM)
SMEM = pl.BlockSpec(memory_space=pltpu.SMEM)
HBM = pl.BlockSpec(memory_space=pltpu.HBM)


def started(position, starts_ref):
    count = jnp.zeros_like(position)
    for i in range(starts_ref.shape[0] - 1):
        count = count + (position >= starts_ref[i]).astype(jnp.int32)
    return count


def cumulative(decay_ref):
    tokens = decay_ref.shape[1]
    i = lax.broadcasted_iota(jnp.int32, (tokens, tokens), 0)
    j = lax.broadcasted_iota(jnp.int32, (tokens, tokens), 1)
    lower = (i >= j).astype(BF16)
    return lax.dot_general(lower, decay_ref[...], (((1,), (1,)), ((), ())), preferred_element_type=F32)


def parts(value):
    high = value.astype(BF16).astype(F32)
    return high, (value - high).astype(BF16).astype(F32)


def rows_of(values, count):
    row = lax.broadcasted_iota(jnp.int32, (count, E), 0)
    tile = jnp.zeros((count, E), F32)
    for n, value in enumerate(values):
        for i, part in enumerate(parts(value)):
            tile = jnp.where(row == 2 * n + i, jnp.broadcast_to(part, (count, E)), tile)
    return tile.astype(BF16)


def value_of(tile, n):
    return tile[2 * n : 2 * n + 1] + tile[2 * n + 1 : 2 * n + 2]


def column(h):
    return slice(h * E, (h + 1) * E)


def summarize(first_ref, starts_ref, k_hbm, v_hbm, decay_ref, out_ref, k_ref, v_ref, piece_ref, in_sems, out_sems):
    heads, tokens = decay_ref.shape
    each = heads // NS
    loads = []
    for n in range(each):
        wide = slice(n * NS * E, (n + 1) * NS * E)
        for i, (source, target) in enumerate(((k_hbm, k_ref), (v_hbm, v_ref))):
            loads.append(pltpu.make_async_copy(source.at[:, wide], target.at[:, wide], in_sems.at[2 * n + i]))
            loads[-1].start()
    first = first_ref[0]
    position = first + lax.broadcasted_iota(jnp.int32, (tokens, 1), 0)
    at_end = started(first + tokens - 1, starts_ref)
    cum = cumulative(decay_ref)
    last = cum[tokens - 1 :, :]
    tail = jnp.where(started(position, starts_ref) == at_end, jnp.exp(last - cum), 0.0)
    open_all = at_end == started(first - 1, starts_ref)
    keep = jnp.where(open_all, jnp.exp(last), 0.0)
    for s in range(NS):
        extra = rows_of([keep[:, n * NS + s : n * NS + s + 1] for n in range(each)], 2 * each)
        for c in range(2):
            piece_ref[c * NS + s, each * HALF :, :] = extra
    copies = []
    for n in range(each):
        loads[2 * n].wait()
        loads[2 * n + 1].wait()
        for s in range(NS):
            h = n * NS + s
            scaled = (k_ref[:, column(h)].astype(F32) * tail[:, h : h + 1]).astype(BF16)
            state = lax.dot_general(
                scaled, v_ref[:, column(h)], (((0,), (0,)), ((), ())), preferred_element_type=F32
            ).astype(BF16)
            for c in range(2):
                piece_ref[c * NS + s, n * HALF : (n + 1) * HALF, :] = state[c * HALF : (c + 1) * HALF]
        end = each * (HALF + 2) if n == each - 1 else (n + 1) * HALF
        block = slice(n * HALF, end)
        copies.append(pltpu.make_async_copy(piece_ref.at[:, block, :], out_ref.at[:, block, :], out_sems.at[n]))
        copies[-1].start()
    for copy in copies:
        copy.wait()


def within(first_ref, starts_ref, q_ref, k_ref, v_ref, decay_ref, out_ref, done_ref):
    done_ref[...] = jnp.zeros_like(done_ref)
    heads, tokens = decay_ref.shape
    first = first_ref[0]
    i = lax.broadcasted_iota(jnp.int32, (tokens, tokens), 0)
    j = lax.broadcasted_iota(jnp.int32, (tokens, tokens), 1)
    mask = (i >= j) & (started(first + i, starts_ref) == started(first + j, starts_ref))
    cum = cumulative(decay_ref)
    across = cum.T
    for h in range(heads):
        scores = lax.dot_general(
            q_ref[:, column(h)], k_ref[:, column(h)], (((1,), (1,)), ((), ())), preferred_element_type=F32
        )
        decay = jnp.exp(jnp.where(mask, cum[:, h : h + 1] - across[h : h + 1, :], -1e30))
        weights = (scores * decay).astype(BF16)
        out_ref[:, column(h)] = jnp.dot(weights, v_ref[:, column(h)], preferred_element_type=F32)


def row_total(near_ref, out_ref):
    sources, rows = near_ref.shape[0], near_ref.shape[1]
    each = rows // (HALF + 2)
    keeps = [near_ref[p, each * HALF :, :].astype(F32) for p in range(sources)]
    for n in range(each):
        totals = []
        for c in range(2):
            state = near_ref[c * NS, n * HALF : (n + 1) * HALF, :].astype(F32)
            total = value_of(keeps[c * NS], n)
            for x in range(1, NS):
                mine = value_of(keeps[c * NS + x], n)
                state = mine * state + near_ref[c * NS + x, n * HALF : (n + 1) * HALF, :].astype(F32)
                total = mine * total
            for z in range(2):
                out_ref[z * each + n, c * QUARTER : (c + 1) * QUARTER, :] = state[
                    z * QUARTER : (z + 1) * QUARTER
                ].astype(BF16)
            totals.append(total)
        extra = rows_of(totals, 8)
        for z in range(2):
            out_ref[z * each + n, HALF:, :] = extra


def in_order(sources):
    each = sources // 2
    return [(z * each + y, c) for z in range(2) for c in range(2) for y in range(each)]


def block_total(middle_ref, out_ref):
    state, total = jnp.zeros((QUARTER, E), F32), jnp.ones((1, E), F32)
    for p, c in in_order(middle_ref.shape[0]):
        mine = value_of(middle_ref[p, HALF:, :].astype(F32), c)
        state = mine * state + middle_ref[p, c * QUARTER : (c + 1) * QUARTER, :].astype(F32)
        total = mine * total
    state, extra = state.astype(BF16), rows_of([total], 8)
    for z in range(out_ref.shape[0]):
        out_ref[z, 0:QUARTER, :] = state
        out_ref[z, QUARTER:, :] = extra


def enter_rows(block_ref, far_ref, middle_ref, gain_ref, _, out_ref):
    def earlier(n, state):
        keep = value_of(far_ref[n, QUARTER:, :].astype(F32), 0)
        return keep * state + far_ref[n, 0:QUARTER, :].astype(F32)

    state = lax.fori_loop(0, block_ref[0], earlier, jnp.zeros((QUARTER, E), F32))
    for p, c in in_order(middle_ref.shape[0]):
        out_ref[p, c * QUARTER : (c + 1) * QUARTER, :] = state.astype(BF16)
        mine = value_of(middle_ref[p, HALF:, :].astype(F32), c)
        state = mine * state + middle_ref[p, c * QUARTER : (c + 1) * QUARTER, :].astype(F32)
    extra = rows_of([gain_ref[...]], 8)
    for p in range(out_ref.shape[0]):
        out_ref[p, HALF:, :] = extra


def enter_chunks(middle_ref, near_ref, out_ref, piece_ref, state_ref, sems):
    sources, rows = near_ref.shape[0], near_ref.shape[1]
    each = rows // (HALF + 2)
    gains = [middle_ref[n, HALF:, :] for n in range(each)]
    copies = []
    for c in range(2):
        for x in range(NS):
            p = c * NS + x
            keeps = near_ref[p, each * HALF :, :].astype(F32)
            for n in range(each):
                if x == 0:
                    state = jnp.concatenate(
                        [
                            middle_ref[z * each + n, c * QUARTER : (c + 1) * QUARTER, :].astype(F32)
                            for z in range(2)
                        ]
                    )
                else:
                    state = state_ref[n]
                piece_ref[p, n * HALF : (n + 1) * HALF, :] = state.astype(BF16)
                piece_ref[p, each * HALF + 2 * n : each * HALF + 2 * n + 2, :] = gains[n][0:2]
                if x < NS - 1:
                    state_ref[n] = value_of(keeps, n) * state + near_ref[
                        p, n * HALF : (n + 1) * HALF, :
                    ].astype(F32)
            copies.append(pltpu.make_async_copy(piece_ref.at[p], out_ref.at[p], sems.at[p]))
            copies[-1].start()
    for copy in copies:
        copy.wait()


def finish(first_ref, starts_ref, q_ref, decay_ref, within_ref, enter_ref, out_hbm, out_ref, sems):
    heads, tokens = decay_ref.shape
    each = heads // NS
    first = first_ref[0]
    position = first + lax.broadcasted_iota(jnp.int32, (tokens, 1), 0)
    opened = started(position, starts_ref) == started(first - 1, starts_ref)
    reach = jnp.where(opened, jnp.exp(cumulative(decay_ref)), 0.0)
    gains = [enter_ref[x, each * HALF :, :].astype(F32) for x in range(NS)]
    copies = []
    for h in range(heads):
        n, x = divmod(h, NS)
        state = jnp.concatenate([enter_ref[c * NS + x, n * HALF : (n + 1) * HALF, :] for c in range(2)], axis=0)
        inter = jnp.dot(q_ref[:, column(h)], state, preferred_element_type=F32)
        attn = within_ref[:, column(h)] + inter * reach[:, h : h + 1]
        meansq = jnp.mean(attn * attn, axis=-1, keepdims=True)
        normed = attn * lax.rsqrt(meansq + 1e-05) * value_of(gains[x], n)
        out_ref[:, column(h)] = normed.astype(BF16)
        if x == NS - 1:
            wide = slice(n * NS * E, (n + 1) * NS * E)
            copies.append(pltpu.make_async_copy(out_ref.at[:, wide], out_hbm.at[:, wide], sems.at[n]))
            copies[-1].start()
    for copy in copies:
        copy.wait()


def call(kernel, out, specs, name, flops, nbytes, limit=None, out_specs=None, scratch=()):
    return pl.pallas_call(
        kernel,
        out_shape=out,
        in_specs=specs,
        out_specs=jax.tree.map(lambda _: VMEM, out) if out_specs is None else out_specs,
        scratch_shapes=scratch,
        name=name,
        compiler_params=pltpu.CompilerParams(vmem_limit_bytes=limit),
        cost_estimate=pl.CostEstimate(flops=flops, bytes_accessed=nbytes, transcendentals=0),
    )


def exchange(value, axes):
    return lax.all_to_all(value, axes, split_axis=0, concat_axis=0, tiled=True)


def per_device(queries, keys, values, log_decay, gain, doc_starts):
    tokens, heads = log_decay.shape
    each = heads // NS
    far = lax.axis_size(FAR)
    first = (lax.axis_index(AXES) * tokens).astype(jnp.int32).reshape(1)
    block = lax.axis_index(FAR).astype(jnp.int32).reshape(1)
    decay = log_decay.T
    shape = jax.ShapeDtypeStruct
    tri = 2 * tokens * tokens * E
    square = 2 * tokens * E * E
    near_shape = (2 * NS, each * (HALF + 2), E)
    middle_shape = (2 * each, HALF + 8, E)
    near_scratch = pltpu.VMEM(near_shape, BF16)
    near_bytes = 2 * 2 * heads * HALF * E

    sent = call(
        summarize, shape(near_shape, BF16), [SMEM, SMEM, HBM, HBM, VMEM], "summarize",
        heads * square, 4 * tokens * heads * E + near_bytes, out_specs=HBM,
        scratch=[
            pltpu.VMEM((tokens, heads * E), BF16), pltpu.VMEM((tokens, heads * E), BF16), near_scratch,
            pltpu.SemaphoreType.DMA((2 * each,)), pltpu.SemaphoreType.DMA((each,)),
        ],
    )(first, doc_starts, keys, values, decay)
    near = exchange(sent, NEAR)

    inside, done = call(
        within, (shape((tokens, heads * E), F32), shape((8, E), F32)),
        [SMEM, SMEM, VMEM, VMEM, VMEM, VMEM], "within", 2 * heads * tri, 10 * tokens * heads * E,
    )(first, doc_starts, queries, keys, values, decay)
    near, done = lax.optimization_barrier((near, done))

    rows = call(
        row_total, shape(middle_shape, BF16), [VMEM], "row_total", 2 * near_bytes, near_bytes, SMALL,
    )(near)
    middle = exchange(rows, MIDDLE)
    total = call(
        block_total, shape((far, QUARTER + 8, E), BF16), [VMEM], "block_total", near_bytes, near_bytes // 4, SMALL,
    )(middle)
    totals = exchange(total, FAR)
    row_states = call(
        enter_rows, shape(middle_shape, BF16), [SMEM, VMEM, VMEM, VMEM, HBM], "enter_rows", near_bytes, near_bytes // 2, SMALL,
    )(block, totals, middle, gain.reshape(1, E), done)
    row_states = exchange(row_states, MIDDLE)
    states = call(
        enter_chunks, shape(near_shape, BF16), [VMEM, VMEM], "enter_chunks", 2 * near_bytes, 2 * near_bytes, SMALL,
        out_specs=HBM,
        scratch=[near_scratch, pltpu.VMEM((each, HALF, E), F32), pltpu.SemaphoreType.DMA((2 * NS,))],
    )(row_states, near)
    states = exchange(states, NEAR)
    return call(
        finish, shape((tokens, heads * E), BF16), [SMEM, SMEM] + [VMEM] * 4, "finish",
        heads * square, 10 * tokens * heads * E, SMALL, out_specs=HBM,
        scratch=[pltpu.VMEM((tokens, heads * E), BF16), pltpu.SemaphoreType.DMA((each,))],
    )(first, doc_starts, queries, decay, inside, states)


def solution(mesh):
    ctx, heads = mesh.devices.shape
    split = Mesh(mesh.devices.reshape(ctx // 4, 2, 2, heads // NS, 2, NS // 2), AXES)
    rows = P(AXES, None)
    return jax.shard_map(
        per_device,
        mesh=split,
        in_specs=(rows, rows, rows, rows, P(("yh", "yl", "x")), P()),
        out_specs=rows,
        check_vma=False,
    )
```

time: 117 us -> 115 us (0.983)
  blocking collectives: 49.7 us -> 69.5 us
  waiting for transfers between devices: 21.2 us -> 8.98 us
  starting transfers between devices: 24.8 us -> 17.7 us
  local copies, waits for them, and re-layouts: 1.83 us -> 0.03 us
    all_to_all x3 -> x4, blocking collectives: 49.7 us -> 69.5 us  [exchange(): return lax.all_to_all(value, axes, split_axis=0, concat_axis=0, tiled=True)]
    all_to_all x2 -> x1, waiting for transfers between devices: 21.2 us -> 8.98 us  [exchange(): return lax.all_to_all(value, axes, split_axis=0, concat_axis=0, tiled=True)]
    all_to_all x2 -> x1, starting transfers between devices: 24.8 us -> 17.7 us  [exchange(): return lax.all_to_all(value, axes, split_axis=0, concat_axis=0, tiled=True)]
    unnamed x14 -> x12, local copies, waits for them, and re-layouts: 1.83 us -> 0.03 us
    pallas_call x6 -> x5, Pallas kernels: 17.5 us -> 16.6 us  [the longest x1 7.54 us: per_device(): call(within, (shape((tokens, heads * E), F32), shape((8, E), F32)), [SMEM...]
  transfers between devices with their start and end apart: 2 -> 1, of which waited for: 2 -> 1; matrix products, arithmetic and copies ran while one was open for 0% -> 0% of each run, Pallas kernels for 8% -> 7%
where the time goes in v3:
time: 115 us
  blocking collectives  69.5 us (60%)
  Pallas kernels  18.5 us (16%)
  starting transfers between devices  17.7 us (15%)
  waiting for transfers between devices  8.98 us (8%)
    all_to_all x4, blocking collectives, exchange(): return lax.all_to_all(value, axes, split_axis=0, concat_axis=0, tiled=True)  69.5 us
    all_to_all x1, starting transfers between devices, exchange(): return lax.all_to_all(value, axes, split_axis=0, concat_axis=0, tiled=True)  17.7 us
    all_to_all x1, waiting for transfers between devices, exchange(): return lax.all_to_all(value, axes, split_axis=0, concat_axis=0, tiled=True)  8.98 us
    pallas_call x1, Pallas kernels, per_device(): call(within, (shape((tokens, heads * E), F32), shape((8, E), F32)), [SMEM...  7.54 us
    pallas_call x1, Pallas kernels, per_device(): call(summarize, shape(near_shape, BF16), [SMEM, SMEM, HBM, HBM, VMEM], 's...  4.54 us
    pallas_call x1, Pallas kernels, per_device(): call(finish, shape((tokens, heads * E), BF16), [SMEM, SMEM] + [VMEM] * 4,...  4.29 us
  transfers between devices with their start and end apart: 1, of which 1 were waited for; matrix products, arithmetic and copies ran while one was open for 0% of the time, Pallas kernels for 7%

profile of v3, /device:TPU:1, one launch (start us, length us, event | category | flops | bytes accessed | tf_op | source)
XLA Modules:
  0.0 114.7 jit_solution(15931088711773289191)
XLA Ops:
  0.0 4.5 %summarize.1 = bf16[16,264,128]{2,1,0:T(8,128)(2,1)} custom-call(s32[1]{0:T(128)} %bitcast.first_ref, s32[9]{0:T(128)} %starts_ref.5, bf16[96,4096]{1,0:T(8,128)(2,1)} %k_hbm.1, bf16[96,4096]{1,0:T(8,128)(2,1)} %v_hbm.1, bf16[32,96]{1,0:T(8,128)(2,1)} %bitcast.4), custom_call_target="tpu_custom_call" | custom-call | flops 100663296 | bytes 2621440 | tf_op jit(solution)/shard_map/summarize/pallas_call | solution.py:262
  4.6 17.7 %all-to-all-start = ((bf16[16,264,128]{2,1,0:T(8,128)(2,1)}), bf16[16,264,128]{2,1,0:T(8,128)(2,1)S(1)}, u32[]{:S(2)}, u32[]{:S(2)}) async-start(bf16[16,264,128]{2,1,0:T(8,128)(2,1)} %summarize.1), calls=%async_computation | async-start | bytes 2162688 | tf_op jit(solution)/shard_map/all_to_all | solution.py:244
  22.2 7.5 %within.1 = (f32[96,4096]{1,0:T(8,128)}, f32[8,128]{1,0:T(8,128)}) custom-call(s32[1]{0:T(128)} %bitcast.first_ref, s32[9]{0:T(128)} %starts_ref.5, bf16[96,4096]{1,0:T(8,128)(2,1)} %q_ref.3, bf16[96,4096]{1,0:T(8,128)(2,1)} %k_hbm.1, bf16[96,4096]{1,0:T(8,128)(2,1)} %v_hbm.1, bf16[32,96]{1,0:T(8,128)(2,1)} %bitcast.5), custom_call_target="tpu_custom_call" | custom-call | flops 150994944 | bytes 3932160 | tf_op jit(solution)/shard_map/within/pallas_call | solution.py:272
  29.8 0.0 copy-start.4
  29.8 0.0 copy-start.5
  29.8 9.0 %all-to-all-done.near_ref = bf16[16,264,128]{2,1,0:T(8,128)(2,1)S(1)} async-done(((bf16[16,264,128]{2,1,0:T(8,128)(2,1)}), bf16[16,264,128]{2,1,0:T(8,128)(2,1)S(1)}, u32[]{:S(2)}, u32[]{:S(2)}) %all-to-all-start) | async-done | bytes 1081376 | tf_op jit(solution)/shard_map/all_to_all | solution.py:244
  38.7 0.2 row_total.1
  39.0 10.4 %all_to_all.25.middle_ref = bf16[8,72,128]{2,1,0:T(8,128)(2,1)S(1)} all-to-all(bf16[8,72,128]{2,1,0:T(8,128)(2,1)S(1)} %row_total.1), channel_id=1, replica_groups=mesh['zh'=8,'zl'=2,'core'=2,'yh'=4,'yl'=2,'x'=4] {'zl','yh'}, dimensions={0} | all-to-all | bytes 294912 | tf_op jit(solution)/shard_map/all_to_all | solution.py:244
  49.4 24.1 %all_to_all.26.far_ref = bf16[8,40,128]{2,1,0:T(8,128)(2,1)S(1)} all-to-all(bf16[8,40,128]{2,1,0:T(8,128)(2,1)S(1)} %block_total.1), channel_id=1, replica_groups=mesh['zh'=8,'zl'=2,'core'=2,'yh'=4,'yl'=2,'x'=4] {'zh'}, dimensions={0} | all-to-all | bytes 163840 | tf_op jit(solution)/shard_map/all_to_all | solution.py:244
  73.4 0.0 copy-done.4
  73.4 0.0 copy-done.5
  73.5 12.0 %all_to_all.27.middle_ref = bf16[8,72,128]{2,1,0:T(8,128)(2,1)S(1)} all-to-all(bf16[8,72,128]{2,1,0:T(8,128)(2,1)S(1)} %enter_rows.1), channel_id=1, replica_groups=mesh['zh'=8,'zl'=2,'core'=2,'yh'=4,'yl'=2,'x'=4] {'zl','yh'}, dimensions={0} | all-to-all | bytes 294912 | tf_op jit(solution)/shard_map/all_to_all | solution.py:244
  85.5 0.0 copy-start.1
  85.5 1.8 %enter_chunks.1 = bf16[16,264,128]{2,1,0:T(8,128)(2,1)S(1)} custom-call(bf16[8,72,128]{2,1,0:T(8,128)(2,1)S(1)} %all_to_all.27.middle_ref, bf16[16,264,128]{2,1,0:T(8,128)(2,1)S(1)} %all-to-all-done.near_ref), custom_call_target="tpu_custom_call" | custom-call | flops 2097152 | bytes 2097152 | tf_op jit(solution)/shard_map/enter_chunks/pallas_call | solution.py:290
  87.3 0.0 copy-start
  87.3 0.0 copy-start.2
  87.3 0.0 copy-start.3
  87.3 23.1 %all_to_all.28.enter_ref = bf16[16,264,128]{2,1,0:T(8,128)(2,1)S(1)} all-to-all(bf16[16,264,128]{2,1,0:T(8,128)(2,1)S(1)} %enter_chunks.1), channel_id=1, replica_groups=mesh['zh'=8,'zl'=2,'core'=2,'yh'=4,'yl'=2,'x'=4] {'core','yl','x'}, dimensions={0} | all-to-all | bytes 2162688 | tf_op jit(solution)/shard_map/all_to_all | solution.py:244
  110.4 0.0 copy-done.1
  110.4 0.0 copy-done
  110.4 0.0 copy-done.2
  110.4 0.0 copy-done.3
  110.4 4.3 %finish.1 = bf16[96,4096]{1,0:T(8,128)(2,1)} custom-call(s32[1]{0:T(128)} %bitcast.first_ref, s32[9]{0:T(128)S(1)} %copy-done.3, bf16[96,4096]{1,0:T(8,128)(2,1)S(1)} %copy-done, bf16[32,96]{1,0:T(8,128)(2,1)S(1)} %bitcast.6, f32[96,4096]{1,0:T(8,128)S(1)} %copy-done.1, bf16[16,264,128]{2,1,0:T(8,128)(2,1)S(1)} %all_to_all.28.enter_ref), custom_call_target="tpu_custom_call" | custom-call | flops 100663296 | bytes 3932160 | tf_op jit(solution)/shard_map/finish/pallas_call | solution.py:296
  (2 shorter events, 0.1 us)
Async XLA Ops:
  4.6 34.2 %all-to-all-start = ((bf16[16,264,128]{2,1,0:T(8,128)(2,1)}), bf16[16,264,128]{2,1,0:T(8,128)(2,1)S(1)}, u32[]{:S(2)}, u32[]{:S(2)}) async-start(bf16[16,264,128]{2,1,0:T(8,128)(2,1)} %summarize.1), calls=%async_computation | async-start | bytes 2162688 | tf_op jit(solution)/shard_map/all_to_all | solution.py:244
  29.8 43.7 %copy-start.4 = (f32[8,128]{1,0:T(8,128)S(1)}, f32[8,128]{1,0:T(8,128)}, u32[]{:S(2)}) copy-start(f32[8,128]{1,0:T(8,128)} %get-tuple-element.12._) | copy-start | bytes 12292
  29.8 43.7 %copy-start.5 = (f32[128]{0:T(128)S(1)}, f32[128]{0:T(128)}, u32[]{:S(2)}) copy-start(f32[128]{0:T(128)} %param.10) | copy-start | bytes 1540
  85.5 25.0 %copy-start.1 = (f32[96,4096]{1,0:T(8,128)S(1)}, f32[96,4096]{1,0:T(8,128)}, u32[]{:S(2)}) copy-start(f32[96,4096]{1,0:T(8,128)} %get-tuple-element.9.within_ref) | copy-start | bytes 4718596
  87.3 23.1 %copy-start = (bf16[96,4096]{1,0:T(8,128)(2,1)S(1)}, bf16[96,4096]{1,0:T(8,128)(2,1)}, u32[]{:S(2)}) copy-start(bf16[96,4096]{1,0:T(8,128)(2,1)} %q_ref.3) | copy-start | bytes 2359300
  87.3 23.1 %copy-start.2 = (bf16[96,32]{0,1:T(8,128)(2,1)S(1)}, bf16[96,32]{0,1:T(8,128)(2,1)}, u32[]{:S(2)}) copy-start(bf16[96,32]{0,1:T(8,128)(2,1)} %param.9) | copy-start | bytes 18436
  87.3 23.1 %copy-start.3 = (s32[9]{0:T(128)S(1)}, s32[9]{0:T(128)}, u32[]{:S(2)}) copy-start(s32[9]{0:T(128)} %starts_ref.5) | copy-start | bytes 112

commit v4 on v3

v4 whole, which is shorter than its diff:
```python
import jax
import jax.numpy as jnp
from jax import lax
from jax.experimental import pallas as pl
from jax.experimental.pallas import tpu as pltpu
from jax.sharding import Mesh, PartitionSpec as P

E = 128
QUARTER = E // 4
PAD = 8
NS = 8
AXES = ("zh", "zl", "core", "yh", "yl", "x")
NEAR = ("yl", "x")
MIDDLE = ("zl", "core", "yh")
FAR = "zh"
F32, BF16 = jnp.float32, jnp.bfloat16
SMALL = 14 << 20
VMEM = pl.BlockSpec(memory_space=pltpu.VMEM)
SMEM = pl.BlockSpec(memory_space=pltpu.SMEM)
HBM = pl.BlockSpec(memory_space=pltpu.HBM)


def started(position, starts_ref):
    count = jnp.zeros_like(position)
    for i in range(starts_ref.shape[0] - 1):
        count = count + (position >= starts_ref[i]).astype(jnp.int32)
    return count


def triangle(tokens, upper):
    i = lax.broadcasted_iota(jnp.int32, (tokens, tokens), 0)
    j = lax.broadcasted_iota(jnp.int32, (tokens, tokens), 1)
    return (i <= j if upper else i >= j).astype(BF16)


def cumulative(decay_ref):
    lower = triangle(decay_ref.shape[1], False)
    return lax.dot_general(lower, decay_ref[...], (((1,), (1,)), ((), ())), preferred_element_type=F32)


def parts(value):
    high = value.astype(BF16).astype(F32)
    return high, (value - high).astype(BF16).astype(F32)


def tile_of(values):
    row = lax.broadcasted_iota(jnp.int32, (PAD, E), 0)
    tile = jnp.zeros((PAD, E), F32)
    for n, value in enumerate(values):
        for i, part in enumerate(parts(value)):
            tile = jnp.where(row == 2 * n + i, jnp.broadcast_to(part, (PAD, E)), tile)
    return tile.astype(BF16)


def value_of(tile, n):
    return tile[2 * n : 2 * n + 1] + tile[2 * n + 1 : 2 * n + 2]


def column(h):
    return slice(h * E, (h + 1) * E)


def summarize(first_ref, starts_ref, k_ref, v_ref, decay_ref, out_ref, piece_ref, sems):
    heads, tokens = decay_ref.shape
    each = heads // NS
    first = first_ref[0]
    position = first + lax.broadcasted_iota(jnp.int32, (1, tokens), 1)
    at_end = started(first + tokens - 1, starts_ref)
    cum = jnp.dot(decay_ref[...], triangle(tokens, True), preferred_element_type=F32)
    last = cum[:, tokens - 1 :]
    tail = jnp.where(started(position, starts_ref) == at_end, jnp.exp(last - cum), 0.0)
    open_all = at_end == started(first - 1, starts_ref)
    keep = jnp.broadcast_to(jnp.where(open_all, jnp.exp(last), 0.0), (heads, E))
    copies = []
    for s in range(NS):
        for n in range(each):
            h = n * NS + s
            scaled = (k_ref[:, column(h)].T.astype(F32) * tail[h : h + 1, :]).astype(BF16)
            state = jnp.dot(scaled, v_ref[:, column(h)], preferred_element_type=F32)
            piece_ref[s, n * E : (n + 1) * E, :] = state.astype(BF16)
        piece_ref[s, each * E :, :] = tile_of([keep[n * NS + s : n * NS + s + 1] for n in range(each)])
        copies.append(pltpu.make_async_copy(piece_ref.at[s], out_ref.at[s], sems.at[s]))
        copies[-1].start()
    for copy in copies:
        copy.wait()


def within(first_ref, starts_ref, q_ref, k_ref, v_ref, decay_ref, out_ref, done_ref):
    done_ref[...] = jnp.zeros_like(done_ref)
    heads, tokens = decay_ref.shape
    first = first_ref[0]
    i = lax.broadcasted_iota(jnp.int32, (tokens, tokens), 0)
    j = lax.broadcasted_iota(jnp.int32, (tokens, tokens), 1)
    mask = (i >= j) & (started(first + i, starts_ref) == started(first + j, starts_ref))
    cum = cumulative(decay_ref)
    across = cum.T
    for h in range(heads):
        scores = lax.dot_general(
            q_ref[:, column(h)], k_ref[:, column(h)], (((1,), (1,)), ((), ())), preferred_element_type=F32
        )
        decay = jnp.exp(jnp.where(mask, cum[:, h : h + 1] - across[h : h + 1, :], -1e30))
        weights = (scores * decay).astype(BF16)
        out_ref[:, column(h)] = jnp.dot(weights, v_ref[:, column(h)], preferred_element_type=F32)


def row_total(near_ref, out_ref):
    each = near_ref.shape[1] // E
    quarters = E // QUARTER
    keeps = [near_ref[s, each * E :, :].astype(F32) for s in range(NS)]
    for n in range(each):
        state, total = near_ref[0, n * E : (n + 1) * E, :].astype(F32), value_of(keeps[0], n)
        for s in range(1, NS):
            mine = value_of(keeps[s], n)
            state = mine * state + near_ref[s, n * E : (n + 1) * E, :].astype(F32)
            total = mine * total
        extra = tile_of([total])
        for r in range(quarters):
            out_ref[r * each + n, 0:QUARTER, :] = state[r * QUARTER : (r + 1) * QUARTER].astype(BF16)
            out_ref[r * each + n, QUARTER:, :] = extra


def after(ref, n, state):
    keep = value_of(ref[n, QUARTER:, :].astype(F32), 0)
    return keep * state + ref[n, 0:QUARTER, :].astype(F32), keep


def block_total(middle_ref, out_ref):
    state, total = jnp.zeros((QUARTER, E), F32), jnp.ones((1, E), F32)
    for n in range(middle_ref.shape[0]):
        state, keep = after(middle_ref, n, state)
        total = keep * total
    state, extra = state.astype(BF16), tile_of([total])
    for z in range(out_ref.shape[0]):
        out_ref[z, 0:QUARTER, :] = state
        out_ref[z, QUARTER:, :] = extra


def enter_rows(block_ref, far_ref, middle_ref, gain_ref, _, out_ref):
    state = lax.fori_loop(
        0, block_ref[0], lambda n, state: after(far_ref, n, state)[0], jnp.zeros((QUARTER, E), F32)
    )
    extra = tile_of([gain_ref[...]])
    for n in range(middle_ref.shape[0]):
        out_ref[n, 0:QUARTER, :] = state.astype(BF16)
        out_ref[n, QUARTER:, :] = extra
        state, _ = after(middle_ref, n, state)


def enter_chunks(middle_ref, near_ref, out_ref):
    each = near_ref.shape[1] // E
    quarters = E // QUARTER
    keeps = [near_ref[s, each * E :, :].astype(F32) for s in range(NS)]
    for n in range(each):
        state = jnp.concatenate([middle_ref[r * each + n, 0:QUARTER, :].astype(F32) for r in range(quarters)])
        for s in range(NS):
            out_ref[s, n * E : (n + 1) * E, :] = state.astype(BF16)
            if s < NS - 1:
                state = value_of(keeps[s], n) * state + near_ref[s, n * E : (n + 1) * E, :].astype(F32)
    row = lax.broadcasted_iota(jnp.int32, (PAD, E), 0)
    gains = jnp.zeros((PAD, E), F32)
    for n in range(each):
        tile = middle_ref[n, QUARTER:, :].astype(F32)
        for i in range(2):
            gains = jnp.where(row == 2 * n + i, jnp.broadcast_to(tile[i : i + 1], (PAD, E)), gains)
    for s in range(NS):
        out_ref[s, each * E :, :] = gains.astype(BF16)


def finish(first_ref, starts_ref, q_ref, decay_ref, within_ref, enter_ref, out_hbm, out_ref, sems):
    heads, tokens = decay_ref.shape
    each = heads // NS
    first = first_ref[0]
    position = first + lax.broadcasted_iota(jnp.int32, (tokens, 1), 0)
    opened = started(position, starts_ref) == started(first - 1, starts_ref)
    reach = jnp.where(opened, jnp.exp(cumulative(decay_ref)), 0.0)
    gains = [enter_ref[s, each * E :, :].astype(F32) for s in range(NS)]
    average = jnp.full((E, E), 1.0 / E, BF16)
    copies = []
    for h in range(heads):
        n, s = divmod(h, NS)
        inter = jnp.dot(q_ref[:, column(h)], enter_ref[s, n * E : (n + 1) * E, :], preferred_element_type=F32)
        attn = within_ref[:, column(h)] + inter * reach[:, h : h + 1]
        meansq = jnp.dot((attn * attn).astype(BF16), average, preferred_element_type=F32)
        normed = attn * lax.rsqrt(meansq + 1e-05) * value_of(gains[s], n)
        out_ref[:, column(h)] = normed.astype(BF16)
        if s == NS - 1:
            wide = slice(n * NS * E, (n + 1) * NS * E)
            copies.append(pltpu.make_async_copy(out_ref.at[:, wide], out_hbm.at[:, wide], sems.at[n]))
            copies[-1].start()
    for copy in copies:
        copy.wait()


def call(kernel, out, specs, name, flops, nbytes, limit=None, out_specs=None, scratch=()):
    return pl.pallas_call(
        kernel,
        out_shape=out,
        in_specs=specs,
        out_specs=jax.tree.map(lambda _: VMEM, out) if out_specs is None else out_specs,
        scratch_shapes=scratch,
        name=name,
        compiler_params=pltpu.CompilerParams(vmem_limit_bytes=limit),
        cost_estimate=pl.CostEstimate(flops=flops, bytes_accessed=nbytes, transcendentals=0),
    )


def exchange(value, axes):
    return lax.all_to_all(value, axes, split_axis=0, concat_axis=0, tiled=True)


def per_device(queries, keys, values, log_decay, gain, doc_starts):
    tokens, heads = log_decay.shape
    each = heads // NS
    far = lax.axis_size(FAR)
    first = (lax.axis_index(AXES) * tokens).astype(jnp.int32).reshape(1)
    block = lax.axis_index(FAR).astype(jnp.int32).reshape(1)
    decay = log_decay.T
    shape = jax.ShapeDtypeStruct
    tri = 2 * tokens * tokens * E
    square = 2 * tokens * E * E
    near_shape = (NS, each * E + PAD, E)
    middle_shape = (4 * each, QUARTER + PAD, E)
    near_bytes = 2 * heads * E * E

    sent = call(
        summarize, shape(near_shape, BF16), [SMEM, SMEM, VMEM, VMEM, VMEM], "summarize",
        heads * square, 4 * tokens * heads * E + near_bytes, out_specs=HBM,
        scratch=[pltpu.VMEM(near_shape, BF16), pltpu.SemaphoreType.DMA((NS,))],
    )(first, doc_starts, keys, values, decay)
    near = exchange(sent, NEAR)

    inside, done = call(
        within, (shape((tokens, heads * E), F32), shape((8, E), F32)),
        [SMEM, SMEM, VMEM, VMEM, VMEM, VMEM], "within", 2 * heads * tri, 10 * tokens * heads * E,
    )(first, doc_starts, queries, keys, values, decay)
    near, done = lax.optimization_barrier((near, done))

    rows = call(
        row_total, shape(middle_shape, BF16), [VMEM], "row_total", 2 * near_bytes, near_bytes, SMALL,
    )(near)
    middle = exchange(rows, MIDDLE)
    total = call(
        block_total, shape((far, QUARTER + PAD, E), BF16), [VMEM], "block_total", near_bytes, near_bytes // 4, SMALL,
    )(middle)
    totals = exchange(total, FAR)
    row_states = call(
        enter_rows, shape(middle_shape, BF16), [SMEM, VMEM, VMEM, VMEM, HBM], "enter_rows", near_bytes, near_bytes // 2, SMALL,
    )(block, totals, middle, gain.reshape(1, E), done)
    row_states = exchange(row_states, MIDDLE)
    states = call(
        enter_chunks, shape(near_shape, BF16), [VMEM, VMEM], "enter_chunks", 2 * near_bytes, 2 * near_bytes, SMALL,
    )(row_states, near)
    states = exchange(states, NEAR)
    return call(
        finish, shape((tokens, heads * E), BF16), [SMEM, SMEM] + [VMEM] * 4, "finish",
        heads * square, 10 * tokens * heads * E, SMALL, out_specs=HBM,
        scratch=[pltpu.VMEM((tokens, heads * E), BF16), pltpu.SemaphoreType.DMA((each,))],
    )(first, doc_starts, queries, decay, inside, states)


def solution(mesh):
    ctx, heads = mesh.devices.shape
    split = Mesh(mesh.devices.reshape(ctx // 4, 2, 2, heads // NS, 2, NS // 2), AXES)
    rows = P(AXES, None)
    return jax.shard_map(
        per_device,
        mesh=split,
        in_specs=(rows, rows, rows, rows, P(("yh", "yl", "x")), P()),
        out_specs=rows,
        check_vma=False,
    )
```

time: 115 us -> 109 us (0.948)
  blocking collectives: 69.5 us -> 87.9 us
  starting transfers between devices: 17.7 us -> 5.86 us
  waiting for transfers between devices: 8.98 us -> 1.99 us
  Pallas kernels: 18.5 us -> 13.2 us
    all_to_all x4, blocking collectives: 69.5 us -> 87.9 us  [exchange(): return lax.all_to_all(value, axes, split_axis=0, concat_axis=0, tiled=True)]
    all_to_all x1, starting transfers between devices: 17.7 us -> 5.86 us  [exchange(): return lax.all_to_all(value, axes, split_axis=0, concat_axis=0, tiled=True)]
    all_to_all x1, waiting for transfers between devices: 8.98 us -> 1.99 us  [exchange(): return lax.all_to_all(value, axes, split_axis=0, concat_axis=0, tiled=True)]
    pallas_call x1, Pallas kernels: 4.29 us -> 2.18 us  [per_device(): call(finish, shape((tokens, heads * E), BF16), [SMEM, SMEM] + [VMEM] * 4,...]
    pallas_call x2, Pallas kernels: 4.59 us -> 3.02 us  [the longest x1 2.96 us: per_device(): call(summarize, shape(near_shape, BF16), [SMEM, SMEM, VMEM, VMEM, VMEM],...]
    pallas_call x1, Pallas kernels: 1.81 us -> 0.24 us  [per_device(): call(enter_chunks, shape(near_shape, BF16), [VMEM, VMEM], 'enter_chunks',...]
where the time goes in v4:
time: 109 us
  blocking collectives  87.9 us (81%)
  Pallas kernels  13.2 us (12%)
  starting transfers between devices  5.86 us (5%)
  waiting for transfers between devices  1.99 us (2%)
    all_to_all x4, blocking collectives, exchange(): return lax.all_to_all(value, axes, split_axis=0, concat_axis=0, tiled=True)  87.9 us
    pallas_call x1, Pallas kernels, per_device(): call(within, (shape((tokens, heads * E), F32), shape((8, E), F32)), [SMEM...  7.54 us
    all_to_all x1, starting transfers between devices, exchange(): return lax.all_to_all(value, axes, split_axis=0, concat_axis=0, tiled=True)  5.86 us
    pallas_call x1, Pallas kernels, per_device(): call(summarize, shape(near_shape, BF16), [SMEM, SMEM, VMEM, VMEM, VMEM],...  2.96 us
    pallas_call x1, Pallas kernels, per_device(): call(finish, shape((tokens, heads * E), BF16), [SMEM, SMEM] + [VMEM] * 4,...  2.18 us
  transfers between devices with their start and end apart: 1, of which 1 were waited for; matrix products, arithmetic and copies ran while one was open for 0% of the time, Pallas kernels for 7%

profile of v4, /device:TPU:1, one launch (start us, length us, event | category | flops | bytes accessed | tf_op | source)
XLA Modules:
  0.0 109.1 jit_solution(4845626637201967636)
XLA Ops:
  0.0 3.0 %summarize.1 = bf16[8,520,128]{2,1,0:T(8,128)(2,1)} custom-call(s32[1]{0:T(128)} %bitcast.first_ref, s32[9]{0:T(128)} %starts_ref.5, bf16[96,4096]{1,0:T(8,128)(2,1)} %k_ref.3, bf16[96,4096]{1,0:T(8,128)(2,1)} %v_ref.3, bf16[32,96]{1,0:T(8,128)(2,1)} %bitcast.4), custom_call_target="tpu_custom_call" | custom-call | flops 100663296 | bytes 2621440 | tf_op jit(solution)/shard_map/summarize/pallas_call | solution.py:225
  3.0 5.9 %all-to-all-start = ((bf16[8,520,128]{2,1,0:T(8,128)(2,1)}), bf16[8,520,128]{2,1,0:T(8,128)(2,1)S(1)}, u32[]{:S(2)}, u32[]{:S(2)}) async-start(bf16[8,520,128]{2,1,0:T(8,128)(2,1)} %summarize.1), calls=%async_computation | async-start | bytes 2129920 | tf_op jit(solution)/shard_map/all_to_all | solution.py:208
  8.8 7.5 %within.1 = (f32[96,4096]{1,0:T(8,128)}, f32[8,128]{1,0:T(8,128)}) custom-call(s32[1]{0:T(128)} %bitcast.first_ref, s32[9]{0:T(128)} %starts_ref.5, bf16[96,4096]{1,0:T(8,128)(2,1)} %q_ref.3, bf16[96,4096]{1,0:T(8,128)(2,1)} %k_ref.3, bf16[96,4096]{1,0:T(8,128)(2,1)} %v_ref.3, bf16[32,96]{1,0:T(8,128)(2,1)} %bitcast.5), custom_call_target="tpu_custom_call" | custom-call | flops 150994944 | bytes 3932160 | tf_op jit(solution)/shard_map/within/pallas_call | solution.py:232
  16.4 0.0 copy-start.4
  16.4 0.0 copy-start.5
  16.4 2.0 %all-to-all-done.near_ref = bf16[8,520,128]{2,1,0:T(8,128)(2,1)S(1)} async-done(((bf16[8,520,128]{2,1,0:T(8,128)(2,1)}), bf16[8,520,128]{2,1,0:T(8,128)(2,1)S(1)}, u32[]{:S(2)}, u32[]{:S(2)}) %all-to-all-start) | async-done | bytes 1064992 | tf_op jit(solution)/shard_map/all_to_all | solution.py:208
  18.4 0.2 row_total.1
  18.6 25.3 %all_to_all.25.middle_ref = bf16[16,40,128]{2,1,0:T(8,128)(2,1)S(1)} all-to-all(bf16[16,40,128]{2,1,0:T(8,128)(2,1)S(1)} %row_total.1), channel_id=1, replica_groups=mesh['zh'=8,'zl'=2,'core'=2,'yh'=4,'yl'=2,'x'=4] {'zl','core','yh'}, dimensions={0} | all-to-all | bytes 327680 | tf_op jit(solution)/shard_map/all_to_all | solution.py:208
  43.8 0.1 block_total.1
  43.9 31.1 %all_to_all.26.far_ref = bf16[8,40,128]{2,1,0:T(8,128)(2,1)S(1)} all-to-all(bf16[8,40,128]{2,1,0:T(8,128)(2,1)S(1)} %block_total.1), channel_id=1, replica_groups=mesh['zh'=8,'zl'=2,'core'=2,'yh'=4,'yl'=2,'x'=4] {'zh'}, dimensions={0} | all-to-all | bytes 163840 | tf_op jit(solution)/shard_map/all_to_all | solution.py:208
  75.0 0.0 copy-done.4
  75.0 0.0 copy-done.5
  75.0 12.6 %all_to_all.27.middle_ref = bf16[16,40,128]{2,1,0:T(8,128)(2,1)S(1)} all-to-all(bf16[16,40,128]{2,1,0:T(8,128)(2,1)S(1)} %enter_rows.1), channel_id=1, replica_groups=mesh['zh'=8,'zl'=2,'core'=2,'yh'=4,'yl'=2,'x'=4] {'zl','core','yh'}, dimensions={0} | all-to-all | bytes 327680 | tf_op jit(solution)/shard_map/all_to_all | solution.py:208
  87.6 0.0 copy-start.1
  87.6 0.2 enter_chunks.1
  87.9 0.0 copy-start
  87.9 0.0 copy-start.2
  87.9 0.0 copy-start.3
  87.9 19.0 %all_to_all.28.enter_ref = bf16[8,520,128]{2,1,0:T(8,128)(2,1)S(1)} all-to-all(bf16[8,520,128]{2,1,0:T(8,128)(2,1)S(1)} %enter_chunks.1), channel_id=1, replica_groups=mesh['zh'=8,'zl'=2,'core'=2,'yh'=4,'yl'=2,'x'=4] {'yl','x'}, dimensions={0} | all-to-all | bytes 2129920 | tf_op jit(solution)/shard_map/all_to_all | solution.py:208
  106.9 0.0 copy-done.1
  106.9 0.0 copy-done
  106.9 0.0 copy-done.2
  106.9 0.0 copy-done.3
  106.9 2.2 %finish.1 = bf16[96,4096]{1,0:T(8,128)(2,1)} custom-call(s32[1]{0:T(128)} %bitcast.first_ref, s32[9]{0:T(128)S(1)} %copy-done.3, bf16[96,4096]{1,0:T(8,128)(2,1)S(1)} %copy-done, bf16[32,96]{1,0:T(8,128)(2,1)S(1)} %bitcast.6, f32[96,4096]{1,0:T(8,128)S(1)} %copy-done.1, bf16[8,520,128]{2,1,0:T(8,128)(2,1)S(1)} %all_to_all.28.enter_ref), custom_call_target="tpu_custom_call" | custom-call | flops 100663296 | bytes 3932160 | tf_op jit(solution)/shard_map/finish/pallas_call | solution.py:254
  (1 shorter events, 0.0 us)
Async XLA Ops:
  3.0 15.4 %all-to-all-start = ((bf16[8,520,128]{2,1,0:T(8,128)(2,1)}), bf16[8,520,128]{2,1,0:T(8,128)(2,1)S(1)}, u32[]{:S(2)}, u32[]{:S(2)}) async-start(bf16[8,520,128]{2,1,0:T(8,128)(2,1)} %summarize.1), calls=%async_computation | async-start | bytes 2129920 | tf_op jit(solution)/shard_map/all_to_all | solution.py:208
  16.4 58.6 %copy-start.4 = (f32[8,128]{1,0:T(8,128)S(1)}, f32[8,128]{1,0:T(8,128)}, u32[]{:S(2)}) copy-start(f32[8,128]{1,0:T(8,128)} %get-tuple-element.12._) | copy-start | bytes 12292
  16.4 58.6 %copy-start.5 = (f32[128]{0:T(128)S(1)}, f32[128]{0:T(128)}, u32[]{:S(2)}) copy-start(f32[128]{0:T(128)} %param.10) | copy-start | bytes 1540
  87.6 19.3 %copy-start.1 = (f32[96,4096]{1,0:T(8,128)S(1)}, f32[96,4096]{1,0:T(8,128)}, u32[]{:S(2)}) copy-start(f32[96,4096]{1,0:T(8,128)} %get-tuple-element.9.within_ref) | copy-start | bytes 4718596
  87.9 19.0 %copy-start = (bf16[96,4096]{1,0:T(8,128)(2,1)S(1)}, bf16[96,4096]{1,0:T(8,128)(2,1)}, u32[]{:S(2)}) copy-start(bf16[96,4096]{1,0:T(8,128)(2,1)} %q_ref.3) | copy-start | bytes 2359300
  87.9 19.0 %copy-start.2 = (bf16[96,32]{0,1:T(8,128)(2,1)S(1)}, bf16[96,32]{0,1:T(8,128)(2,1)}, u32[]{:S(2)}) copy-start(bf16[96,32]{0,1:T(8,128)(2,1)} %param.9) | copy-start | bytes 18436
  87.9 19.0 %copy-start.3 = (s32[9]{0:T(128)S(1)}, s32[9]{0:T(128)}, u32[]{:S(2)}) copy-start(s32[9]{0:T(128)} %starts_ref.5) | copy-start | bytes 112

commit v5 on v4

--- a/solution.py
+++ b/solution.py
@@ -9,6 +9,7 @@
 QUARTER = E // 4
 PAD = 8
 NS = 8
+BLOCK_ROWS = 2 * E + PAD
 AXES = ("zh", "zl", "core", "yh", "yl", "x")
 NEAR = ("yl", "x")
 MIDDLE = ("zl", "core", "yh")
@@ -40,29 +41,42 @@
 
 def parts(value):
     high = value.astype(BF16).astype(F32)
-    return high, (value - high).astype(BF16).astype(F32)
-
-
-def tile_of(values):
+    middle = (value - high).astype(BF16).astype(F32)
+    return high, middle, (value - high - middle).astype(BF16).astype(F32)
+
+
+def tile_of(values, count=3):
     row = lax.broadcasted_iota(jnp.int32, (PAD, E), 0)
     tile = jnp.zeros((PAD, E), F32)
     for n, value in enumerate(values):
-        for i, part in enumerate(parts(value)):
-            tile = jnp.where(row == 2 * n + i, jnp.broadcast_to(part, (PAD, E)), tile)
+        for i, part in enumerate(parts(value)[:count]):
+            tile = jnp.where(row == count * n + i, jnp.broadcast_to(part, (PAD, E)), tile)
     return tile.astype(BF16)
 
 
-def value_of(tile, n):
-    return tile[2 * n : 2 * n + 1] + tile[2 * n + 1 : 2 * n + 2]
+def value_of(tile, n, count=3):
+    value = tile[count * n : count * n + 1]
+    for i in range(1, count):
+        value = value + tile[count * n + i : count * n + i + 1]
+    return value
+
+
+def rows_at(n):
+    start = (n // 2) * BLOCK_ROWS + (n % 2) * E
+    return slice(start, start + E)
+
+
+def keep_in(near_ref, s, n):
+    start = (n // 2) * BLOCK_ROWS + 2 * E
+    return value_of(near_ref[s, start : start + PAD, :].astype(F32), n % 2)
 
 
 def column(h):
     return slice(h * E, (h + 1) * E)
 
 
-def summarize(first_ref, starts_ref, k_ref, v_ref, decay_ref, out_ref, piece_ref, sems):
+def summarize(first_ref, starts_ref, k_ref, v_ref, decay_ref, out_ref):
     heads, tokens = decay_ref.shape
-    each = heads // NS
     first = first_ref[0]
     position = first + lax.broadcasted_iota(jnp.int32, (1, tokens), 1)
     at_end = started(first + tokens - 1, starts_ref)
@@ -71,18 +85,13 @@
     tail = jnp.where(started(position, starts_ref) == at_end, jnp.exp(last - cum), 0.0)
     open_all = at_end == started(first - 1, starts_ref)
     keep = jnp.broadcast_to(jnp.where(open_all, jnp.exp(last), 0.0), (heads, E))
-    copies = []
     for s in range(NS):
-        for n in range(each):
+        for n in range(2):
             h = n * NS + s
             scaled = (k_ref[:, column(h)].T.astype(F32) * tail[h : h + 1, :]).astype(BF16)
             state = jnp.dot(scaled, v_ref[:, column(h)], preferred_element_type=F32)
-            piece_ref[s, n * E : (n + 1) * E, :] = state.astype(BF16)
-        piece_ref[s, each * E :, :] = tile_of([keep[n * NS + s : n * NS + s + 1] for n in range(each)])
-        copies.append(pltpu.make_async_copy(piece_ref.at[s], out_ref.at[s], sems.at[s]))
-        copies[-1].start()
-    for copy in copies:
-        copy.wait()
+            out_ref[s, n * E : (n + 1) * E, :] = state.astype(BF16)
+        out_ref[s, 2 * E :, :] = tile_of([keep[n * NS + s : n * NS + s + 1] for n in range(2)])
 
 
 def within(first_ref, starts_ref, q_ref, k_ref, v_ref, decay_ref, out_ref, done_ref):
@@ -104,14 +113,13 @@
 
 
 def row_total(near_ref, out_ref):
-    each = near_ref.shape[1] // E
     quarters = E // QUARTER
-    keeps = [near_ref[s, each * E :, :].astype(F32) for s in range(NS)]
+    each = out_ref.shape[0] // quarters
     for n in range(each):
-        state, total = near_ref[0, n * E : (n + 1) * E, :].astype(F32), value_of(keeps[0], n)
+        state, total = near_ref[0, rows_at(n), :].astype(F32), keep_in(near_ref, 0, n)
         for s in range(1, NS):
-            mine = value_of(keeps[s], n)
-            state = mine * state + near_ref[s, n * E : (n + 1) * E, :].astype(F32)
+            mine = keep_in(near_ref, s, n)
+            state = mine * state + near_ref[s, rows_at(n), :].astype(F32)
             total = mine * total
         extra = tile_of([total])
         for r in range(quarters):
@@ -139,7 +147,7 @@
     state = lax.fori_loop(
         0, block_ref[0], lambda n, state: after(far_ref, n, state)[0], jnp.zeros((QUARTER, E), F32)
     )
-    extra = tile_of([gain_ref[...]])
+    extra = tile_of([gain_ref[...]], 2)
     for n in range(middle_ref.shape[0]):
         out_ref[n, 0:QUARTER, :] = state.astype(BF16)
         out_ref[n, QUARTER:, :] = extra
@@ -147,15 +155,14 @@
 
 
 def enter_chunks(middle_ref, near_ref, out_ref):
-    each = near_ref.shape[1] // E
     quarters = E // QUARTER
-    keeps = [near_ref[s, each * E :, :].astype(F32) for s in range(NS)]
+    each = middle_ref.shape[0] // quarters
     for n in range(each):
         state = jnp.concatenate([middle_ref[r * each + n, 0:QUARTER, :].astype(F32) for r in range(quarters)])
         for s in range(NS):
             out_ref[s, n * E : (n + 1) * E, :] = state.astype(BF16)
             if s < NS - 1:
-                state = value_of(keeps[s], n) * state + near_ref[s, n * E : (n + 1) * E, :].astype(F32)
+                state = keep_in(near_ref, s, n) * state + near_ref[s, rows_at(n), :].astype(F32)
     row = lax.broadcasted_iota(jnp.int32, (PAD, E), 0)
     gains = jnp.zeros((PAD, E), F32)
     for n in range(each):
@@ -181,7 +188,7 @@
         inter = jnp.dot(q_ref[:, column(h)], enter_ref[s, n * E : (n + 1) * E, :], preferred_element_type=F32)
         attn = within_ref[:, column(h)] + inter * reach[:, h : h + 1]
         meansq = jnp.dot((attn * attn).astype(BF16), average, preferred_element_type=F32)
-        normed = attn * lax.rsqrt(meansq + 1e-05) * value_of(gains[s], n)
+        normed = attn * lax.rsqrt(meansq + 1e-05) * value_of(gains[s], n, 2)
         out_ref[:, column(h)] = normed.astype(BF16)
         if s == NS - 1:
             wide = slice(n * NS * E, (n + 1) * NS * E)
@@ -191,10 +198,11 @@
         copy.wait()
 
 
-def call(kernel, out, specs, name, flops, nbytes, limit=None, out_specs=None, scratch=()):
+def call(kernel, out, specs, name, flops, nbytes, limit=None, out_specs=None, scratch=(), grid=()):
     return pl.pallas_call(
         kernel,
         out_shape=out,
+        grid=grid,
         in_specs=specs,
         out_specs=jax.tree.map(lambda _: VMEM, out) if out_specs is None else out_specs,
         scratch_shapes=scratch,
@@ -218,14 +226,17 @@
     shape = jax.ShapeDtypeStruct
     tri = 2 * tokens * tokens * E
     square = 2 * tokens * E * E
-    near_shape = (NS, each * E + PAD, E)
+    up_shape = (NS, each // 2 * BLOCK_ROWS, E)
+    down_shape = (NS, each * E + PAD, E)
     middle_shape = (4 * each, QUARTER + PAD, E)
     near_bytes = 2 * heads * E * E
+    some = pl.BlockSpec((tokens, 2 * NS * E), lambda i: (0, i))
 
     sent = call(
-        summarize, shape(near_shape, BF16), [SMEM, SMEM, VMEM, VMEM, VMEM], "summarize",
-        heads * square, 4 * tokens * heads * E + near_bytes, out_specs=HBM,
-        scratch=[pltpu.VMEM(near_shape, BF16), pltpu.SemaphoreType.DMA((NS,))],
+        summarize, shape(up_shape, BF16),
+        [SMEM, SMEM, some, some, pl.BlockSpec((2 * NS, tokens), lambda i: (i, 0))], "summarize",
+        heads * square, 4 * tokens * heads * E + near_bytes, grid=(each // 2,),
+        out_specs=pl.BlockSpec((NS, BLOCK_ROWS, E), lambda i: (0, i, 0)),
     )(first, doc_starts, keys, values, decay)
     near = exchange(sent, NEAR)
 
@@ -248,7 +259,7 @@
     )(block, totals, middle, gain.reshape(1, E), done)
     row_states = exchange(row_states, MIDDLE)
     states = call(
-        enter_chunks, shape(near_shape, BF16), [VMEM, VMEM], "enter_chunks", 2 * near_bytes, 2 * near_bytes, SMALL,
+        enter_chunks, shape(down_shape, BF16), [VMEM, VMEM], "enter_chunks", 2 * near_bytes, 2 * near_bytes, SMALL,
     )(row_states, near)
     states = exchange(states, NEAR)
     return call(

time: 109 us -> 110 us (level)
  no operation moved by 1% of the time
where the time goes in v5:
time: 110 us; the launch traced here: 109 us
  blocking collectives  88 us (80%)
  Pallas kernels  13.3 us (12%)
  starting transfers between devices  5.86 us (5%)
  waiting for transfers between devices  2.07 us (2%)
    all_to_all x4, blocking collectives, exchange(): return lax.all_to_all(value, axes, split_axis=0, concat_axis=0, tiled=True)  88 us
    pallas_call x1, Pallas kernels, per_device(): call(within, (shape((tokens, heads * E), F32), shape((8, E), F32)), [SMEM...  7.54 us
    all_to_all x1, starting transfers between devices, exchange(): return lax.all_to_all(value, axes, split_axis=0, concat_axis=0, tiled=True)  5.86 us
    pallas_call x1, Pallas kernels, per_device(): call(summarize, shape(up_shape, BF16), [SMEM, SMEM, some, some, pl.BlockS...  3 us
  transfers between devices with their start and end apart: 1, of which 1 were waited for; matrix products, arithmetic and copies ran while one was open for 0% of the time, Pallas kernels for 7%

profile of v5, /device:TPU:1, one launch (start us, length us, event | category | flops | bytes accessed | tf_op | source)
XLA Modules:
  0.0 109.3 jit_solution(14480844569920409300)
XLA Ops:
  0.0 3.0 %summarize.1 = bf16[8,528,128]{2,1,0:T(8,128)(2,1)} custom-call(s32[1]{0:T(128)} %bitcast.first_ref, s32[9]{0:T(128)} %starts_ref.5, bf16[96,4096]{1,0:T(8,128)(2,1)} %k_ref.3, bf16[96,4096]{1,0:T(8,128)(2,1)} %v_ref.3, bf16[32,96]{1,0:T(8,128)(2,1)} %bitcast.4), custom_call_target="tpu_custom_call" | custom-call | flops 100663296 | bytes 2621440 | tf_op jit(solution)/shard_map/summarize/pallas_call | solution.py:235
  3.0 5.9 %all-to-all-start = ((bf16[8,528,128]{2,1,0:T(8,128)(2,1)}), bf16[8,528,128]{2,1,0:T(8,128)(2,1)S(1)}, u32[]{:S(2)}, u32[]{:S(2)}) async-start(bf16[8,528,128]{2,1,0:T(8,128)(2,1)} %summarize.1), calls=%async_computation | async-start | bytes 2162688 | tf_op jit(solution)/shard_map/all_to_all | solution.py:216
  8.9 7.5 %within.1 = (f32[96,4096]{1,0:T(8,128)}, f32[8,128]{1,0:T(8,128)}) custom-call(s32[1]{0:T(128)} %bitcast.first_ref, s32[9]{0:T(128)} %starts_ref.5, bf16[96,4096]{1,0:T(8,128)(2,1)} %q_ref.3, bf16[96,4096]{1,0:T(8,128)(2,1)} %k_ref.3, bf16[96,4096]{1,0:T(8,128)(2,1)} %v_ref.3, bf16[32,96]{1,0:T(8,128)(2,1)} %bitcast.5), custom_call_target="tpu_custom_call" | custom-call | flops 150994944 | bytes 3932160 | tf_op jit(solution)/shard_map/within/pallas_call | solution.py:243
  16.4 0.0 copy-start.4
  16.4 0.0 copy-start.5
  16.4 2.1 %all-to-all-done.near_ref = bf16[8,528,128]{2,1,0:T(8,128)(2,1)S(1)} async-done(((bf16[8,528,128]{2,1,0:T(8,128)(2,1)}), bf16[8,528,128]{2,1,0:T(8,128)(2,1)S(1)}, u32[]{:S(2)}, u32[]{:S(2)}) %all-to-all-start) | async-done | bytes 1081376 | tf_op jit(solution)/shard_map/all_to_all | solution.py:216
  18.5 0.2 row_total.1
  18.7 25.2 %all_to_all.25.middle_ref = bf16[16,40,128]{2,1,0:T(8,128)(2,1)S(1)} all-to-all(bf16[16,40,128]{2,1,0:T(8,128)(2,1)S(1)} %row_total.1), channel_id=1, replica_groups=mesh['zh'=8,'zl'=2,'core'=2,'yh'=4,'yl'=2,'x'=4] {'zl','core','yh'}, dimensions={0} | all-to-all | bytes 327680 | tf_op jit(solution)/shard_map/all_to_all | solution.py:216
  44.0 0.1 block_total.1
  44.0 31.2 %all_to_all.26.far_ref = bf16[8,40,128]{2,1,0:T(8,128)(2,1)S(1)} all-to-all(bf16[8,40,128]{2,1,0:T(8,128)(2,1)S(1)} %block_total.1), channel_id=1, replica_groups=mesh['zh'=8,'zl'=2,'core'=2,'yh'=4,'yl'=2,'x'=4] {'zh'}, dimensions={0} | all-to-all | bytes 163840 | tf_op jit(solution)/shard_map/all_to_all | solution.py:216
  75.2 0.0 copy-done.4
  75.2 0.0 copy-done.5
  75.2 12.6 %all_to_all.27.middle_ref = bf16[16,40,128]{2,1,0:T(8,128)(2,1)S(1)} all-to-all(bf16[16,40,128]{2,1,0:T(8,128)(2,1)S(1)} %enter_rows.1), channel_id=1, replica_groups=mesh['zh'=8,'zl'=2,'core'=2,'yh'=4,'yl'=2,'x'=4] {'zl','core','yh'}, dimensions={0} | all-to-all | bytes 327680 | tf_op jit(solution)/shard_map/all_to_all | solution.py:216
  87.8 0.0 copy-start.1
  87.8 0.3 enter_chunks.1
  88.1 0.0 copy-start
  88.1 0.0 copy-start.2
  88.1 0.0 copy-start.3
  88.2 19.0 %all_to_all.28.enter_ref = bf16[8,520,128]{2,1,0:T(8,128)(2,1)S(1)} all-to-all(bf16[8,520,128]{2,1,0:T(8,128)(2,1)S(1)} %enter_chunks.1), channel_id=1, replica_groups=mesh['zh'=8,'zl'=2,'core'=2,'yh'=4,'yl'=2,'x'=4] {'yl','x'}, dimensions={0} | all-to-all | bytes 2129920 | tf_op jit(solution)/shard_map/all_to_all | solution.py:216
  107.1 0.0 copy-done.1
  107.1 0.0 copy-done
  107.1 0.0 copy-done.2
  107.1 0.0 copy-done.3
  107.2 2.2 %finish.1 = bf16[96,4096]{1,0:T(8,128)(2,1)} custom-call(s32[1]{0:T(128)} %bitcast.first_ref, s32[9]{0:T(128)S(1)} %copy-done.3, bf16[96,4096]{1,0:T(8,128)(2,1)S(1)} %copy-done, bf16[32,96]{1,0:T(8,128)(2,1)S(1)} %bitcast.6, f32[96,4096]{1,0:T(8,128)S(1)} %copy-done.1, bf16[8,520,128]{2,1,0:T(8,128)(2,1)S(1)} %all_to_all.28.enter_ref), custom_call_target="tpu_custom_call" | custom-call | flops 100663296 | bytes 3932160 | tf_op jit(solution)/shard_map/finish/pallas_call | solution.py:265
  (1 shorter events, 0.0 us)
Async XLA Ops:
  3.0 15.5 %all-to-all-start = ((bf16[8,528,128]{2,1,0:T(8,128)(2,1)}), bf16[8,528,128]{2,1,0:T(8,128)(2,1)S(1)}, u32[]{:S(2)}, u32[]{:S(2)}) async-start(bf16[8,528,128]{2,1,0:T(8,128)(2,1)} %summarize.1), calls=%async_computation | async-start | bytes 2162688 | tf_op jit(solution)/shard_map/all_to_all | solution.py:216
  16.4 58.8 %copy-start.4 = (f32[8,128]{1,0:T(8,128)S(1)}, f32[8,128]{1,0:T(8,128)}, u32[]{:S(2)}) copy-start(f32[8,128]{1,0:T(8,128)} %get-tuple-element.12._) | copy-start | bytes 12292
  16.4 58.8 %copy-start.5 = (f32[128]{0:T(128)S(1)}, f32[128]{0:T(128)}, u32[]{:S(2)}) copy-start(f32[128]{0:T(128)} %param.10) | copy-start | bytes 1540
  87.8 19.3 %copy-start.1 = (f32[96,4096]{1,0:T(8,128)S(1)}, f32[96,4096]{1,0:T(8,128)}, u32[]{:S(2)}) copy-start(f32[96,4096]{1,0:T(8,128)} %get-tuple-element.9.within_ref) | copy-start | bytes 4718596
  88.1 19.0 %copy-start = (bf16[96,4096]{1,0:T(8,128)(2,1)S(1)}, bf16[96,4096]{1,0:T(8,128)(2,1)}, u32[]{:S(2)}) copy-start(bf16[96,4096]{1,0:T(8,128)(2,1)} %q_ref.3) | copy-start | bytes 2359300
  88.1 19.0 %copy-start.2 = (bf16[96,32]{0,1:T(8,128)(2,1)S(1)}, bf16[96,32]{0,1:T(8,128)(2,1)}, u32[]{:S(2)}) copy-start(bf16[96,32]{0,1:T(8,128)(2,1)} %param.9) | copy-start | bytes 18436
  88.1 19.0 %copy-start.3 = (s32[9]{0:T(128)S(1)}, s32[9]{0:T(128)}, u32[]{:S(2)}) copy-start(s32[9]{0:T(128)} %starts_ref.5) | copy-start | bytes 112
